TPU v7x, 128 devices: a whole 4x4x4 slice. The times are simulated.
128 devices in a mesh: fsdp: 2 (over core), expert: 64 (over z, y, x).
Axes of the slice: x: 4, y: 4, z: 4, core: 2. Of those that a mesh axis runs over, the one named last changes fastest.
Arguments:
- tokens: bfloat16 [8192, 4096], P(('fsdp', 'expert')), may hold values from -6 to 6
- expert_ids: int32 [8192, 8], P(('fsdp', 'expert')), may hold values from 0 to 63, all different within a row; in each aligned block of 64 rows (0 to 63, 64 to 127, ...) at most 9 rows name the same one
- route_weight: float32 [8192, 8], P(('fsdp', 'expert')), may hold values from 0.1 to 1
- gate_weight: bfloat16 [64, 768, 4096], P('expert', 'fsdp'), may hold values from -0.09375 to 0.09375
- up_weight: bfloat16 [64, 768, 4096], P('expert', 'fsdp'), may hold values from -0.09375 to 0.09375
- down_weight: bfloat16 [64, 768, 4096], P('expert', None, 'fsdp'), may hold values from -0.21875 to 0.21875
Outputs:
- mixed: bfloat16 [8192, 4096], P(('fsdp', 'expert'))
Inputs may be any that keep to these rules, and one draw needn't show every extreme that they name: `expert_ids`: each row names 8 different experts; within the rows of one device no expert is named by more than 9 rows, a bound that some block reaches.
All inputs are finite; a program needn't handle non-finite values.
Results may differ from a plain program's by a relative error of at most 0.011.
Values may be sent and summed in bfloat16 or wider, within the bound.
No kernel may reach another device: no remote copies, remote signals or barrier semaphores. Data moves between devices by JAX's collectives and lax.ppermute only.
A program may use at most 128 MiB of HBM per device.

v0:
```python
import jax
import jax.numpy as jnp
from jax import lax
from jax.sharding import PartitionSpec as P


def routing_tables(expert_ids, route_weight, experts_count, capacity):
    tok_count, top_count = expert_ids.shape
    flat_ids = expert_ids.reshape(-1)
    onehot = (flat_ids[:, None] == jnp.arange(experts_count, dtype=jnp.int32)[None, :]).astype(
        jnp.int32
    )
    rank_of = jnp.cumsum(onehot, axis=0) - onehot
    slot_of = jnp.sum(rank_of * onehot, axis=1)
    target = flat_ids * capacity + slot_of
    placed = target[:, None] == jnp.arange(experts_count * capacity, dtype=jnp.int32)[None, :]
    picker = placed.astype(jnp.bfloat16)
    weighted = placed.astype(jnp.float32) * route_weight.reshape(-1)[:, None]
    combine = jnp.sum(weighted.reshape(tok_count, top_count, -1), axis=1)
    return (picker, combine)


def split_table(table):
    upper_part = table.astype(jnp.bfloat16)
    lower_part = (table - upper_part.astype(jnp.float32)).astype(jnp.bfloat16)
    return (upper_part, lower_part)


def project_rows(rows_in, weight_rows):
    return jnp.einsum("sd,fd->sf", rows_in, weight_rows, preferred_element_type=jnp.float32)


def body(tokens, expert_ids, route_weight, gate_weight, up_weight, down_weight):
    groups = lax.axis_size("fsdp")
    experts_count = lax.axis_size("expert") * gate_weight.shape[0]
    tok_count, top_count = expert_ids.shape
    model_width = tokens.shape[1]
    capacity = max(2, tok_count * top_count // experts_count + 1)
    picker, combine = routing_tables(expert_ids, route_weight, experts_count, capacity)
    repeated = jnp.repeat(tokens, top_count, axis=0)
    outgoing = jnp.einsum("aj,ad->jd", picker, repeated, preferred_element_type=jnp.float32).astype(
        jnp.bfloat16
    )
    outgoing = outgoing.reshape(experts_count, capacity, model_width)
    arrived = lax.all_to_all(outgoing, "expert", split_axis=0, concat_axis=0, tiled=True).reshape(
        -1, model_width
    )
    slots_count = arrived.shape[0]
    down_local = down_weight[0]
    gate_part = project_rows(arrived, lax.all_gather(gate_weight, "fsdp", axis=1, tiled=True)[0])
    up_part = project_rows(arrived, lax.all_gather(up_weight, "fsdp", axis=1, tiled=True)[0])
    hidden = (jax.nn.silu(gate_part) * up_part).astype(jnp.bfloat16)
    result = jnp.dot(
        lax.all_gather(hidden, "fsdp", axis=0, tiled=True),
        down_local,
        preferred_element_type=jnp.float32,
    )
    expert_out = result.astype(jnp.bfloat16)
    column_count = expert_out.shape[1]
    own_rows = lax.all_to_all(
        expert_out.reshape(groups, slots_count, column_count),
        "fsdp",
        split_axis=0,
        concat_axis=2,
        tiled=True,
    )
    own_rows = own_rows.reshape(experts_count, capacity, model_width)
    returned = lax.all_to_all(own_rows, "expert", split_axis=0, concat_axis=0, tiled=True).reshape(
        slots_count, model_width
    )
    upper_part, lower_part = split_table(combine)
    mixed = jnp.dot(upper_part, returned, preferred_element_type=jnp.float32) + jnp.dot(
        lower_part, returned, preferred_element_type=jnp.float32
    )
    return mixed.astype(jnp.bfloat16)


def solution(mesh):
    placed = (
        P(("fsdp", "expert"), None),
        P(("fsdp", "expert"), None),
        P(("fsdp", "expert"), None),
        P("expert", "fsdp", None),
        P("expert", "fsdp", None),
        P("expert", None, "fsdp"),
    )
    return jax.shard_map(
        body, mesh=mesh, in_specs=placed, out_specs=P(("fsdp", "expert"), None), check_vma=False
    )
```

profile of v0, /device:TPU:1, one launch (start us, length us, event | category | flops | bytes accessed | tf_op | source)
XLA Modules:
  0.0 358.1 jit_solution(5326400258929450952)
XLA Ops:
  6.5 0.0 copy-start
  6.5 0.0 copy-start.2
  6.5 0.0 all-gather.4.cloned.1.call-start
  6.5 0.7 all-gather.4.cloned.1.call-update
  7.3 0.0 all-gather.6.cloned.1.call-start
  7.3 0.7 all-gather.6.cloned.1.call-update
  8.0 0.0 all-gather.8.cloned.1.call-start
  8.1 0.0 copy-done.2
  8.1 0.1 copy.30
  8.2 0.1 eq.49
  8.2 0.1 eq.45
  8.4 1.2 reduce-window.6
  9.6 0.2 slice_reduce_fusion
  9.8 0.1 fusion.13
  10.0 5.5 %convolution_convert_fusion.1 = bf16[576,4096]{1,0:T(8,128)(2,1)} fusion(bf16[64,4096]{1,0:T(8,128)(2,1)} %param.6, s32[512]{0:T(512)S(1)} %multiply_add_fusion.1), kind=kOutput, calls=%fused_computation.5 | convolution fusion | flops 2418573312 | bytes 5244928 | tf_op jit(solution)/shard_map/aj,ad->jd/dot_general | solution.py:41
  15.5 8.3 %reshape.63 = bf16[64,9,4096]{2,1,0:T(8,128)(2,1)} reshape(bf16[576,4096]{1,0:T(8,128)(2,1)} %convolution_convert_fusion.1) | data formatting | bytes 9437184 | tf_op jit(solution)/shard_map/reshape | solution.py:44
  23.8 110.6 %all_to_all.25 = bf16[64,9,4096]{2,1,0:T(8,128)(2,1)} all-to-all(bf16[64,9,4096]{2,1,0:T(8,128)(2,1)} %reshape.63), channel_id=1, replica_groups=mesh['fsdp'=2,'expert'=64] {'expert'}, dimensions={0} | all-to-all | bytes 9437184 | tf_op jit(solution)/shard_map/all_to_all | solution.py:45
  134.4 8.5 %reshape.64 = bf16[576,4096]{1,0:T(8,128)(2,1)} reshape(bf16[64,9,4096]{2,1,0:T(8,128)(2,1)} %all_to_all.25) | data formatting | bytes 9437184 | tf_op jit(solution)/shard_map/reshape | solution.py:45
  142.9 0.0 all-gather.4.cloned.1.call-done
  142.9 9.3 %fusion.2 = f32[576,768]{1,0:T(8,128)} fusion(bf16[576,4096]{1,0:T(8,128)(2,1)} %reshape.64, bf16[1,768,4096]{2,1,0:T(8,128)(2,1)} %all-gather.4.cloned.1.call-done), kind=kOutput, calls=%fused_computation.3 | convolution fusion | flops 3623878656 | bytes 12779520 | tf_op jit(solution)/shard_map/sd,fd->sf/dot_general | solution.py:30
  152.2 0.0 all-gather.6.cloned.1.call-done
  152.2 9.5 %multiply_convert_fusion = bf16[576,768]{1,0:T(8,128)(2,1)} fusion(f32[576,768]{1,0:T(8,128)} %fusion.2, bf16[576,4096]{1,0:T(8,128)(2,1)} %reshape.64, bf16[1,768,4096]{2,1,0:T(8,128)(2,1)} %all-gather.6.cloned.1.call-done), kind=kOutput, calls=%fused_computation.11 | convolution fusion | flops 3626532864 | bytes 13664256 | tf_op jit(solution)/shard_map/sd,fd->sf/dot_general | solution.py:30
  161.8 0.0 all-gather.8.cloned.1.call-update
  161.8 9.9 %all-gather.8.cloned.1.call-done = bf16[1152,768]{1,0:T(8,128)(2,1)} async-done(((bf16[576,768]{1,0:T(8,128)(2,1)}), bf16[1152,768]{1,0:T(8,128)(2,1)}) %all-gather.8.cloned.1.call-update) | async-done | bytes 1769488 | tf_op jit(solution)/shard_map/all_gather | solution.py:54
  171.7 0.0 copy-done
  171.7 5.5 %convolution_convert_fusion = bf16[1152,2048]{1,0:T(8,128)(2,1)S(1)} fusion(bf16[1152,768]{1,0:T(8,128)(2,1)} %all-gather.8.cloned.1.call-done, bf16[1,768,2048]{2,1,0:T(8,128)(2,1)S(1)} %copy-done), kind=kOutput, calls=%fused_computation | convolution fusion | flops 3626237952 | bytes 9633792 | tf_op jit(solution)/shard_map/dot_general | solution.py:53
  177.2 8.5 %all_to_all.26 = bf16[2,576,2048]{2,1,0:T(8,128)(2,1)} all-to-all(bf16[2,576,2048]{2,1,0:T(8,128)(2,1)S(1)} %bitcast.43), channel_id=1, replica_groups=mesh['fsdp'=2,'expert'=64] {'fsdp'}, dimensions={0} | all-to-all | bytes 9437184 | tf_op jit(solution)/shard_map/all_to_all | solution.py:60
  185.8 9.3 %copy.36 = bf16[1,576,2,2048]{3,2,1,0:T(2,128)(2,1)} copy(bf16[1,576,2,2048]{3,1,2,0:T(8,128)(2,1)} %bitcast.42) | data formatting | bytes 9437184 | tf_op jit(solution)/shard_map/all_to_all | solution.py:60
  195.1 14.1 %reshape.66 = bf16[64,9,4096]{2,1,0:T(8,128)(2,1)} reshape(bf16[1,576,2,2048]{3,2,1,0:T(2,128)(2,1)} %copy.36) | data formatting | bytes 9437184 | tf_op jit(solution)/shard_map/reshape | solution.py:67
  209.2 0.0 copy-start.3
  209.2 10.5 %all-to-all-start.2 = ((bf16[64,9,4096]{2,1,0:T(8,128)(2,1)}), bf16[64,9,4096]{2,1,0:T(8,128)(2,1)}, u32[]{:S(2)}, u32[]{:S(2)}) async-start(bf16[64,9,4096]{2,1,0:T(8,128)(2,1)} %reshape.66), calls=%async_computation.2 | async-start | bytes 16777216 | tf_op jit(solution)/shard_map/all_to_all | solution.py:68
  219.7 0.1 reduce_sum.21
  219.8 0.1 copy.33
  219.9 0.1 copy.34
  220.0 0.0 copy-done.3
  220.0 0.1 copy.35
  220.0 0.5 select_reduce_fusion
  220.5 117.0 %all-to-all-done.2 = bf16[64,9,4096]{2,1,0:T(8,128)(2,1)} async-done(((bf16[64,9,4096]{2,1,0:T(8,128)(2,1)}), bf16[64,9,4096]{2,1,0:T(8,128)(2,1)}, u32[]{:S(2)}, u32[]{:S(2)}) %all-to-all-start.2) | async-done | bytes 4718624 | tf_op jit(solution)/shard_map/all_to_all | solution.py:68
  337.5 8.4 %reshape.67 = bf16[576,4096]{1,0:T(8,128)(2,1)} reshape(bf16[64,9,4096]{2,1,0:T(8,128)(2,1)} %all-to-all-done.2) | data formatting | bytes 9437184 | tf_op jit(solution)/shard_map/reshape | solution.py:68
  346.0 0.0 copy-start.1
  346.0 3.5 fusion.16
  349.5 0.3 copy-done.1
  349.7 1.8 fusion.4
  (5 shorter events, 0.1 us)
Async XLA Ops:
  6.5 165.2 %copy-start = (bf16[1,768,2048]{2,1,0:T(8,128)(2,1)S(1)}, bf16[1,768,2048]{2,1,0:T(8,128)(2,1)}, u32[]{:S(2)}) copy-start(bf16[1,768,2048]{2,1,0:T(8,128)(2,1)} %param.11) | copy-start | bytes 9437188
  6.5 1.5 copy-start.2
  6.5 136.4 %all-gather.4.cloned.1.call-start = ((), (), s32[]{:S(2)}) async-start(), calls=%async_computation.3 | async-start | bytes 9437184 | tf_op jit(solution)/shard_map/all_gather | solution.py:50
  7.3 145.0 %all-gather.6.cloned.1.call-start = ((), (), s32[]{:S(2)}) async-start(), calls=%async_computation.4 | async-start | bytes 9437184 | tf_op jit(solution)/shard_map/all_gather | solution.py:51
  8.0 163.7 %all-gather.8.cloned.1.call-start = ((), (), s32[]{:S(2)}) async-start(), calls=%async_computation.5 | async-start | bytes 2654208 | tf_op jit(solution)/shard_map/all_gather | solution.py:54
  209.2 10.8 %copy-start.3 = (f32[64,8]{0,1:T(8,128)S(1)}, f32[64,8]{0,1:T(8,128)}, u32[]{:S(2)}) copy-start(f32[64,8]{0,1:T(8,128)} %param.8) | copy-start | bytes 6148
  209.2 128.3 %all-to-all-start.2 = ((bf16[64,9,4096]{2,1,0:T(8,128)(2,1)}), bf16[64,9,4096]{2,1,0:T(8,128)(2,1)}, u32[]{:S(2)}, u32[]{:S(2)}) async-start(bf16[64,9,4096]{2,1,0:T(8,128)(2,1)} %reshape.66), calls=%async_computation.2 | async-start | bytes 16777216 | tf_op jit(solution)/shard_map/all_to_all | solution.py:68
  346.0 3.8 %copy-start.1 = (bf16[576,4096]{1,0:T(8,128)(2,1)S(1)}, bf16[576,4096]{1,0:T(8,128)(2,1)}, u32[]{:S(2)}) copy-start(bf16[576,4096]{1,0:T(8,128)(2,1)} %reshape.67) | copy-start | bytes 14155780
Sparse Core Ops, SparseCore 0:
  9.0 23.1 all-gather.3
  33.8 20.7 all-gather.5
  161.9 9.7 all-gather.7
where the time goes:
time: 364 us; the launch traced here: 358 us
  waiting for transfers between devices  128 us (35%)
  blocking collectives  119 us (33%)
  local copies, waits for them, and re-layouts  49.7 us (14%)
  matrix products  35.2 us (10%)
  between operations  13.2 us (4%)
  starting transfers between devices  10.6 us (3%)
    all_to_all x1, waiting for transfers between devices, body(): lax.all_to_all(own_rows, 'expert', split_axis=0, concat_axis=0, tiled=True)  117 us
    all_to_all x1, blocking collectives, body(): lax.all_to_all(outgoing, 'expert', split_axis=0, concat_axis=0, tiled=True)  111 us
    dot_general x2, matrix products, project_rows(): jnp.einsum('sd,fd->sf', rows_in, weight_rows, preferred_element_type=jnp....  18.8 us
    reshape x1, local copies, waits for them, and re-layouts, body(): own_rows = own_rows.reshape(experts_count, capacity, model_width)  14.1 us
    all_to_all x1, starting transfers between devices, body(): lax.all_to_all(own_rows, 'expert', split_axis=0, concat_axis=0, tiled=True)  10.5 us
    all_gather x1, waiting for transfers between devices, body(): lax.all_gather(hidden, 'fsdp', axis=0, tiled=True)  9.95 us
    all_to_all x1, local copies, waits for them, and re-layouts, body(): lax.all_to_all(expert_out.reshape(groups, slots_count, column_count), 'fs...  9.31 us
    all_to_all x1, blocking collectives, body(): lax.all_to_all(expert_out.reshape(groups, slots_count, column_count), 'fs...  8.54 us
  transfers between devices with their start and end apart: 4, of which 2 were waited for; matrix products, arithmetic and copies ran while one was open for 10% of the time, Pallas kernels for 0%

commit v1 on v0

v1 whole, which is shorter than its diff:
```python
import jax
import jax.numpy as jnp
from jax import lax
from jax.sharding import PartitionSpec as P

LANES = 128
CUTS = (0, 4, 9)


def routing_tables(expert_ids, experts_count):
    tok_count, top_count = expert_ids.shape
    names = jnp.arange(experts_count, dtype=jnp.int32)
    chosen = (expert_ids[:, :, None] == names[None, None, :]).astype(jnp.float32)
    by_token = jnp.sum(chosen, axis=1)
    earlier = jnp.arange(tok_count)[:, None] > jnp.arange(tok_count)[None, :]
    rank_of = jnp.dot(earlier.astype(jnp.bfloat16), by_token.astype(jnp.bfloat16),
                      preferred_element_type=jnp.float32)
    return by_token, rank_of


def swap_join(part, axis):
    other = lax.ppermute(part, "fsdp", [(0, 1), (1, 0)])
    first = lax.axis_index("fsdp") == 0
    return jnp.concatenate(
        [jnp.where(first, part, other), jnp.where(first, other, part)], axis=axis)


def body(tokens, expert_ids, route_weight, gate_weight, up_weight, down_weight):
    experts_count = lax.axis_size("expert") * gate_weight.shape[0]
    tok_count, top_count = expert_ids.shape
    width = tokens.shape[1]
    gate_full = swap_join(gate_weight[0], 0)
    up_full = swap_join(up_weight[0], 0)
    down_full = swap_join(down_weight[0], 1)
    by_token, rank_of = routing_tables(expert_ids, experts_count)
    names = jnp.arange(experts_count, dtype=jnp.int32)
    share = jnp.sum(
        jnp.where(expert_ids[:, :, None] == names, route_weight[:, :, None], 0.0), axis=1)

    def table(values, low, high):
        slots = jnp.arange(low, high, dtype=jnp.float32)
        hit = (rank_of[:, :, None] == slots) & (by_token[:, :, None] > 0)
        return jnp.where(hit, values[:, :, None], 0.0).reshape(tok_count, -1).astype(jnp.bfloat16)

    def exchange(rows, count):
        sent = rows.reshape(experts_count, count * width // LANES, LANES)
        came = lax.all_to_all(sent, "expert", split_axis=0, concat_axis=0, tiled=True)
        return came.reshape(experts_count * count, width)

    def dispatch(low, high):
        picker = table(jnp.ones_like(by_token), low, high)
        rows = jnp.einsum("tj,td->jd", picker, tokens,
                          preferred_element_type=jnp.float32).astype(jnp.bfloat16)
        return exchange(rows, high - low)

    def expert(rows):
        gate = jnp.einsum("sd,fd->sf", rows, gate_full, preferred_element_type=jnp.float32)
        up = jnp.einsum("sd,fd->sf", rows, up_full, preferred_element_type=jnp.float32)
        hidden = (jax.nn.silu(gate) * up).astype(jnp.bfloat16)
        return jnp.dot(hidden, down_full,
                       preferred_element_type=jnp.float32).astype(jnp.bfloat16)

    spans = list(zip(CUTS[:-1], CUTS[1:]))
    arrived = [dispatch(low, high) for low, high in spans]
    total = jnp.zeros((tok_count, width), jnp.float32)
    for (low, high), rows in zip(spans, arrived):
        back = exchange(expert(rows), high - low)
        total = total + jnp.dot(table(share, low, high), back, preferred_element_type=jnp.float32)
    return total.astype(jnp.bfloat16)


def solution(mesh):
    placed = (
        P(("fsdp", "expert"), None),
        P(("fsdp", "expert"), None),
        P(("fsdp", "expert"), None),
        P("expert", "fsdp", None),
        P("expert", "fsdp", None),
        P("expert", None, "fsdp"),
    )
    return jax.shard_map(
        body, mesh=mesh, in_specs=placed, out_specs=P(("fsdp", "expert"), None), check_vma=False
    )
```

time: 364 us -> 181 us (0.50)
  blocking collectives: 119 us -> 0 us
  waiting for transfers between devices: 128 us -> 49.4 us
  starting transfers between devices: 10.6 us -> 40 us
  local copies, waits for them, and re-layouts: 49.7 us -> 33.5 us
  between operations: 13.2 us -> 0.19 us
  other arithmetic: 1.87 us -> 13.9 us
  matrix products: 35.2 us -> 41.5 us
    all_to_all x2 -> x0, blocking collectives: 119 us -> none  [the longest x1 111 us: body(): lax.all_to_all(outgoing, 'expert', split_axis=0, concat_axis=0, tiled=True)]
    all_to_all x1 -> x4, waiting for transfers between devices: 117 us -> 49.4 us  [exchange(): lax.all_to_all(sent, 'expert', split_axis=0, concat_axis=0, tiled=True)]
    all_to_all x1 -> x4, starting transfers between devices: 10.5 us -> 37.8 us  [exchange(): lax.all_to_all(sent, 'expert', split_axis=0, concat_axis=0, tiled=True)]
    select_n x0 -> x3, other arithmetic: none -> 13.4 us  [swap_join(): jnp.where(first, part, other)]
    all_gather x3 -> x0, waiting for transfers between devices: 9.95 us -> none  [the longest x1 9.95 us: body(): lax.all_gather(hidden, 'fsdp', axis=0, tiled=True)]
    reshape x4 -> x8, local copies, waits for them, and re-layouts: 39.3 us -> 29.7 us  [the longest x4 15.1 us: exchange(): sent = rows.reshape(experts_count, count * width // LANES, LANES)]
    all_to_all x1 -> x0, local copies, waits for them, and re-layouts: 9.31 us -> none  [body(): lax.all_to_all(expert_out.reshape(groups, slots_count, column_count), 'fs...]
    dot_general x6 -> x9, matrix products: 35.2 us -> 41.5 us  [the longest x2 23.5 us: expert(): jnp.dot(hidden, down_full, preferred_element_type=jnp.float32)]
  transfers between devices with their start and end apart: 4 -> 7, of which waited for: 2 -> 3; matrix products, arithmetic and copies ran while one was open for 10% -> 45% of each run, Pallas kernels for 0% -> 0%
where the time goes in v1:
time: 181 us; the launch traced here: 179 us
  waiting for transfers between devices  49.4 us (27%)
  matrix products  41.5 us (23%)
  starting transfers between devices  40 us (22%)
  local copies, waits for them, and re-layouts  33.5 us (19%)
  other arithmetic  13.9 us (8%)
    all_to_all x4, waiting for transfers between devices, exchange(): lax.all_to_all(sent, 'expert', split_axis=0, concat_axis=0, tiled=True)  49.4 us
    all_to_all x4, starting transfers between devices, exchange(): lax.all_to_all(sent, 'expert', split_axis=0, concat_axis=0, tiled=True)  37.8 us
    dot_general x2, matrix products, expert(): jnp.dot(hidden, down_full, preferred_element_type=jnp.float32)  23.5 us
    reshape x4, local copies, waits for them, and re-layouts, exchange(): sent = rows.reshape(experts_count, count * width // LANES, LANES)  15.1 us
    reshape x4, local copies, waits for them, and re-layouts, exchange(): return came.reshape(experts_count * count, width)  14.6 us
    select_n x3, other arithmetic, swap_join(): jnp.where(first, part, other)  13.4 us
    dot_general x2, matrix products, expert(): jnp.einsum('sd,fd->sf', rows, up_full, preferred_element_type=jnp.float32)  9.67 us
    dot_general x2, matrix products, body(): jnp.dot(table(share, low, high), back, preferred_element_type=jnp.float32)  6.56 us
  transfers between devices with their start and end apart: 7, of which 3 were waited for; matrix products, arithmetic and copies ran while one was open for 45% of the time, Pallas kernels for 0%

profile of v1, /device:TPU:1, one launch (start us, length us, event | category | flops | bytes accessed | tf_op | source)
XLA Modules:
  0.0 178.6 jit_solution(4741797124475718353)
XLA Ops:
  0.0 0.0 copy-start
  0.0 1.4 collective-permute-start.2
  1.4 0.0 collective-permute-start.1
  1.4 0.8 copy.13
  2.2 0.8 copy.16
  3.0 0.2 convert_reduce_fusion
  3.2 0.2 fusion.14
  3.4 0.1 copy.15
  3.5 0.1 eq.111
  3.7 0.0 copy-done
  3.7 0.7 convolution_convert_fusion.2
  4.5 2.4 %reshape.128 = bf16[64,128,128]{2,1,0:T(8,128)(2,1)} reshape(bf16[256,4096]{1,0:T(8,128)(2,1)S(1)} %convolution_convert_fusion.2) | data formatting | bytes 4194304 | tf_op jit(solution)/shard_map/reshape | solution.py:46
  6.9 11.6 %all-to-all-start = ((bf16[64,128,128]{2,1,0:T(8,128)(2,1)}), bf16[64,128,128]{2,1,0:T(8,128)(2,1)}, u32[]{:S(2)}, u32[]{:S(2)}) async-start(bf16[64,128,128]{2,1,0:T(8,128)(2,1)} %reshape.128), calls=%async_computation | async-start | bytes 4194304 | tf_op jit(solution)/shard_map/all_to_all | solution.py:47
  18.4 0.8 collective-permute-start
  19.2 0.1 eq.120
  19.4 0.1 and.57
  19.5 0.9 convolution_convert_fusion.1
  20.4 3.2 %reshape.132 = bf16[64,160,128]{2,1,0:T(8,128)(2,1)} reshape(bf16[320,4096]{1,0:T(8,128)(2,1)S(1)} %convolution_convert_fusion.1) | data formatting | bytes 5242880 | tf_op jit(solution)/shard_map/reshape | solution.py:46
  23.6 23.5 %all-to-all-done = bf16[64,128,128]{2,1,0:T(8,128)(2,1)} async-done(((bf16[64,128,128]{2,1,0:T(8,128)(2,1)}), bf16[64,128,128]{2,1,0:T(8,128)(2,1)}, u32[]{:S(2)}, u32[]{:S(2)}) %all-to-all-start) | async-done | bytes 2097184 | tf_op jit(solution)/shard_map/all_to_all | solution.py:47
  47.1 7.0 %all-to-all-start.2 = ((bf16[64,160,128]{2,1,0:T(8,128)(2,1)}), bf16[64,160,128]{2,1,0:T(8,128)(2,1)S(1)}, u32[]{:S(2)}, u32[]{:S(2)}) async-start(bf16[64,160,128]{2,1,0:T(8,128)(2,1)} %reshape.132), calls=%async_computation.2 | async-start | bytes 5242880 | tf_op jit(solution)/shard_map/all_to_all | solution.py:47
  54.2 4.2 %reshape.129 = bf16[256,4096]{1,0:T(8,128)(2,1)} reshape(bf16[64,128,128]{2,1,0:T(8,128)(2,1)} %all-to-all-done) | data formatting | bytes 4194304 | tf_op jit(solution)/shard_map/reshape | solution.py:48
  58.4 0.0 copy-start.2
  58.4 0.0 collective-permute-done.2
  58.4 6.1 %broadcast_select_fusion.1 = (bf16[768,2048]{1,0:T(8,128)(2,1)}, bf16[768,2048]{1,0:T(8,128)(2,1)}) fusion(bf16[768,2048]{1,0:T(8,128)(2,1)} %collective-permute-done.2, pred[]{:T(512)S(6)} %eq.114, bf16[1,768,2048]{2,1,0:T(8,128)(2,1)} %param.11), kind=kLoop, calls=%fused_computation.14 | loop fusion | flops 3145728 | bytes 12582913 | tf_op jit(solution)/shard_map/jit(_where)/select_n | solution.py:25
  64.5 0.0 copy-start.7
  64.5 0.0 collective-permute-done.1
  64.5 0.0 copy-done.2
  64.5 2.4 %broadcast_select_fusion.3 = (bf16[384,4096]{1,0:T(8,128)(2,1)S(1)}, bf16[384,4096]{1,0:T(8,128)(2,1)S(1)}) fusion(bf16[384,4096]{1,0:T(8,128)(2,1)} %collective-permute-done.1, pred[]{:T(512)S(6)} %eq.114, bf16[1,384,4096]{2,1,0:T(8,128)(2,1)S(1)} %copy-done.2), kind=kLoop, calls=%fused_computation.16 | loop fusion | flops 3145728 | bytes 12582913 | tf_op jit(solution)/shard_map/jit(_where)/select_n | solution.py:25
  66.9 0.0 copy-start.4
  66.9 0.0 copy-start.5
  66.9 0.1 copy-done.7
  67.0 0.0 copy-start.3
  67.0 2.7 %fusion.2 = f32[256,768]{1,0:T(8,128)} fusion(bf16[256,4096]{1,0:T(8,128)(2,1)S(1)} %copy-done.7, bf16[384,4096]{1,0:T(8,128)(2,1)S(1)} %get-tuple-element.10, bf16[384,4096]{1,0:T(8,128)(2,1)S(1)} %get-tuple-element.9), kind=kOutput, calls=%fused_computation.10 | convolution fusion | flops 1623195648 | bytes 9175040 | tf_op jit(solution)/shard_map/sd,fd->sf/dot_general | solution.py:58
  69.7 0.0 copy-done.4
  69.7 0.7 copy-done.5
  70.4 0.0 collective-permute-done
  70.4 0.8 copy-done.3
  71.2 4.9 %broadcast_select_fusion.5 = (bf16[384,4096]{1,0:T(8,128)(2,1)}, bf16[384,4096]{1,0:T(8,128)(2,1)}) fusion(bf16[384,4096]{1,0:T(8,128)(2,1)} %collective-permute-done, pred[]{:T(512)S(6)} %eq.114, bf16[1,384,4096]{2,1,0:T(8,128)(2,1)S(1)} %copy-done.3), kind=kLoop, calls=%fused_computation.18 | loop fusion | flops 3145728 | bytes 12582913 | tf_op jit(solution)/shard_map/jit(_where)/select_n | solution.py:25
  76.1 11.4 %convolution_convert_fusion.3 = bf16[256,4096]{1,0:T(8,128)(2,1)} fusion(bf16[768,2048]{1,0:T(8,128)(2,1)} %get-tuple-element.12, bf16[768,2048]{1,0:T(8,128)(2,1)} %get-tuple-element.11, f32[256,768]{1,0:T(8,128)} %fusion.2, bf16[256,4096]{1,0:T(8,128)(2,1)} %reshape.129, bf16[384,4096]{1,0:T(8,128)(2,1)} %get-tuple-element.8, ...), kind=kOutput, calls=%fused_computation.6 | convolution fusion | flops 3248619520 | bytes 17563648 | tf_op jit(solution)/shard_map/dot_general | solution.py:60
  87.6 4.3 %reshape.130 = bf16[64,128,128]{2,1,0:T(8,128)(2,1)} reshape(bf16[256,4096]{1,0:T(8,128)(2,1)} %convolution_convert_fusion.3) | data formatting | bytes 4194304 | tf_op jit(solution)/shard_map/reshape | solution.py:46
  91.8 0.0 all-to-all-done.2
  91.8 10.1 %all-to-all-start.1 = ((bf16[64,128,128]{2,1,0:T(8,128)(2,1)}), bf16[64,128,128]{2,1,0:T(8,128)(2,1)}, u32[]{:S(2)}, u32[]{:S(2)}) async-start(bf16[64,128,128]{2,1,0:T(8,128)(2,1)} %reshape.130), calls=%async_computation.1 | async-start | bytes 4194304 | tf_op jit(solution)/shard_map/all_to_all | solution.py:47
  101.9 3.1 %reshape.133 = bf16[320,4096]{1,0:T(8,128)(2,1)} reshape(bf16[64,160,128]{2,1,0:T(8,128)(2,1)S(1)} %all-to-all-done.2) | data formatting | bytes 5242880 | tf_op jit(solution)/shard_map/reshape | solution.py:48
  105.0 0.0 copy-start.6
  105.0 6.9 %fusion.1 = f32[320,768]{1,0:T(8,128)} fusion(bf16[320,4096]{1,0:T(8,128)(2,1)} %reshape.133, bf16[384,4096]{1,0:T(8,128)(2,1)} %copy-done.5, bf16[384,4096]{1,0:T(8,128)(2,1)} %copy-done.4), kind=kOutput, calls=%fused_computation.9 | convolution fusion | flops 2025848832 | bytes 9895936 | tf_op jit(solution)/shard_map/sd,fd->sf/dot_general | solution.py:58
  112.0 0.0 copy-done.6
  112.0 12.1 %convolution_convert_fusion = bf16[320,4096]{1,0:T(8,128)(2,1)} fusion(bf16[768,2048]{1,0:T(8,128)(2,1)} %get-tuple-element.12, bf16[768,2048]{1,0:T(8,128)(2,1)} %get-tuple-element.11, f32[320,768]{1,0:T(8,128)} %fusion.1, bf16[320,4096]{1,0:T(8,128)(2,1)S(1)} %copy-done.6, bf16[384,4096]{1,0:T(8,128)(2,1)} %get-tuple-element.8, ...), kind=kOutput, calls=%fused_computation.3 | convolution fusion | flops 4054482944 | bytes 18808832 | tf_op jit(solution)/shard_map/dot_general | solution.py:60
  124.0 5.3 %reshape.134 = bf16[64,160,128]{2,1,0:T(8,128)(2,1)} reshape(bf16[320,4096]{1,0:T(8,128)(2,1)} %convolution_convert_fusion) | data formatting | bytes 5242880 | tf_op jit(solution)/shard_map/reshape | solution.py:46
  129.3 0.4 all-to-all-done.1
  129.7 9.1 %all-to-all-start.3 = ((bf16[64,160,128]{2,1,0:T(8,128)(2,1)}), bf16[64,160,128]{2,1,0:T(8,128)(2,1)S(1)}, u32[]{:S(2)}, u32[]{:S(2)}) async-start(bf16[64,160,128]{2,1,0:T(8,128)(2,1)} %reshape.134), calls=%async_computation.3 | async-start | bytes 5242880 | tf_op jit(solution)/shard_map/all_to_all | solution.py:47
  138.8 0.1 copy.17
  138.9 0.1 select_convert_fusion
  139.1 0.1 convert_element_type.67
  139.1 0.1 select_convert_fusion.3
  139.2 4.2 %reshape.131 = bf16[256,4096]{1,0:T(8,128)(2,1)} reshape(bf16[64,128,128]{2,1,0:T(8,128)(2,1)} %all-to-all-done.1) | data formatting | bytes 4194304 | tf_op jit(solution)/shard_map/reshape | solution.py:48
  143.4 3.1 %fusion.28 = f32[64,4096]{1,0:T(8,128)} fusion(bf16[64,256]{0,1:T(8,128)(2,1)S(1)} %bitcast.32, bf16[256,4096]{1,0:T(8,128)(2,1)} %reshape.131), kind=kOutput, calls=%fused_computation.53 | convolution fusion | flops 134217728 | bytes 3178496 | tf_op jit(solution)/shard_map/dot_general | solution.py:68
  146.5 25.5 %all-to-all-done.3 = bf16[64,160,128]{2,1,0:T(8,128)(2,1)S(1)} async-done(((bf16[64,160,128]{2,1,0:T(8,128)(2,1)}), bf16[64,160,128]{2,1,0:T(8,128)(2,1)S(1)}, u32[]{:S(2)}, u32[]{:S(2)}) %all-to-all-start.3) | async-done | bytes 2621472 | tf_op jit(solution)/shard_map/all_to_all | solution.py:47
  172.0 0.0 copy-start.1
  172.0 3.1 %reshape.135 = bf16[320,4096]{1,0:T(8,128)(2,1)} reshape(bf16[64,160,128]{2,1,0:T(8,128)(2,1)S(1)} %all-to-all-done.3) | data formatting | bytes 5242880 | tf_op jit(solution)/shard_map/reshape | solution.py:48
  175.1 3.5 %fusion = bf16[64,4096]{1,0:T(8,128)(2,1)} fusion(f32[64,4096]{1,0:T(8,128)} %fusion.28, bf16[64,320]{0,1:T(8,128)(2,1)S(1)} %convert_element_type.67, bf16[320,4096]{1,0:T(8,128)(2,1)} %reshape.135), kind=kOutput, calls=%fused_computation.8 | convolution fusion | flops 168296448 | bytes 4235264 | tf_op jit(solution)/shard_map/dot_general | solution.py:68
  178.6 0.0 copy-done.1
  (9 shorter events, 0.2 us)
Async XLA Ops:
  0.0 3.7 %copy-start = (bf16[64,4096]{1,0:T(8,128)(2,1)S(1)}, bf16[64,4096]{1,0:T(8,128)(2,1)}, u32[]{:S(2)}) copy-start(bf16[64,4096]{1,0:T(8,128)(2,1)} %param.6) | copy-start | bytes 1572868
  0.0 58.4 %collective-permute-start.2 = (bf16[768,2048]{1,0:T(8,128)(2,1)}, bf16[768,2048]{1,0:T(8,128)(2,1)}, u32[]{:S(2)}, u32[]{:S(2)}) collective-permute-start(bf16[768,2048]{1,0:T(8,128)(2,1)} %bitcast.28), channel_id=1, source_target_pairs={{0,64},{64,0},{1,65},{65,1},{2,66},{66,2},{3,67},{67,3},{4,68},{68... | collective-permute-start | bytes 9437192 | tf_op jit(solution)/shard_map/ppermute | solution.py:22
  1.4 63.0 %collective-permute-start.1 = (bf16[384,4096]{1,0:T(8,128)(2,1)}, bf16[384,4096]{1,0:T(8,128)(2,1)}, u32[]{:S(2)}, u32[]{:S(2)}) collective-permute-start(bf16[384,4096]{1,0:T(8,128)(2,1)} %bitcast.29), channel_id=1, source_target_pairs={{0,64},{64,0},{1,65},{65,1},{2,66},{66,2},{3,67},{67,3},{4,68},{68... | collective-permute-start | bytes 9437192 | tf_op jit(solution)/shard_map/ppermute | solution.py:22
  6.9 40.3 %all-to-all-start = ((bf16[64,128,128]{2,1,0:T(8,128)(2,1)}), bf16[64,128,128]{2,1,0:T(8,128)(2,1)}, u32[]{:S(2)}, u32[]{:S(2)}) async-start(bf16[64,128,128]{2,1,0:T(8,128)(2,1)} %reshape.128), calls=%async_computation | async-start | bytes 4194304 | tf_op jit(solution)/shard_map/all_to_all | solution.py:47
  18.4 52.0 %collective-permute-start = (bf16[384,4096]{1,0:T(8,128)(2,1)}, bf16[384,4096]{1,0:T(8,128)(2,1)}, u32[]{:S(2)}, u32[]{:S(2)}) collective-permute-start(bf16[384,4096]{1,0:T(8,128)(2,1)} %bitcast.30), channel_id=1, source_target_pairs={{0,64},{64,0},{1,65},{65,1},{2,66},{66,2},{3,67},{67,3},{4,68},{68... | collective-permute-start | bytes 9437192 | tf_op jit(solution)/shard_map/ppermute | solution.py:22
  47.1 44.7 %all-to-all-start.2 = ((bf16[64,160,128]{2,1,0:T(8,128)(2,1)}), bf16[64,160,128]{2,1,0:T(8,128)(2,1)S(1)}, u32[]{:S(2)}, u32[]{:S(2)}) async-start(bf16[64,160,128]{2,1,0:T(8,128)(2,1)} %reshape.132), calls=%async_computation.2 | async-start | bytes 5242880 | tf_op jit(solution)/shard_map/all_to_all | solution.py:47
  58.4 6.1 %copy-start.2 = (bf16[1,384,4096]{2,1,0:T(8,128)(2,1)S(1)}, bf16[1,384,4096]{2,1,0:T(8,128)(2,1)}, u32[]{:S(2)}) copy-start(bf16[1,384,4096]{2,1,0:T(8,128)(2,1)} %param.10) | copy-start | bytes 9437188
  64.5 2.5 %copy-start.7 = (bf16[256,4096]{1,0:T(8,128)(2,1)S(1)}, bf16[256,4096]{1,0:T(8,128)(2,1)}, u32[]{:S(2)}) copy-start(bf16[256,4096]{1,0:T(8,128)(2,1)} %reshape.129) | copy-start | bytes 6291460
  66.9 2.8 %copy-start.4 = (bf16[384,4096]{1,0:T(8,128)(2,1)}, bf16[384,4096]{1,0:T(8,128)(2,1)S(1)}, u32[]{:S(2)}) copy-start(bf16[384,4096]{1,0:T(8,128)(2,1)S(1)} %get-tuple-element.9) | copy-start | bytes 9437188
  66.9 3.5 %copy-start.5 = (bf16[384,4096]{1,0:T(8,128)(2,1)}, bf16[384,4096]{1,0:T(8,128)(2,1)S(1)}, u32[]{:S(2)}) copy-start(bf16[384,4096]{1,0:T(8,128)(2,1)S(1)} %get-tuple-element.10) | copy-start | bytes 9437188
  67.0 4.2 %copy-start.3 = (bf16[1,384,4096]{2,1,0:T(8,128)(2,1)S(1)}, bf16[1,384,4096]{2,1,0:T(8,128)(2,1)}, u32[]{:S(2)}) copy-start(bf16[1,384,4096]{2,1,0:T(8,128)(2,1)} %param.9) | copy-start | bytes 9437188
  91.8 37.8 %all-to-all-start.1 = ((bf16[64,128,128]{2,1,0:T(8,128)(2,1)}), bf16[64,128,128]{2,1,0:T(8,128)(2,1)}, u32[]{:S(2)}, u32[]{:S(2)}) async-start(bf16[64,128,128]{2,1,0:T(8,128)(2,1)} %reshape.130), calls=%async_computation.1 | async-start | bytes 4194304 | tf_op jit(solution)/shard_map/all_to_all | solution.py:47
  105.0 6.9 %copy-start.6 = (bf16[320,4096]{1,0:T(8,128)(2,1)S(1)}, bf16[320,4096]{1,0:T(8,128)(2,1)}, u32[]{:S(2)}) copy-start(bf16[320,4096]{1,0:T(8,128)(2,1)} %reshape.133) | copy-start | bytes 7864324
  129.7 42.3 %all-to-all-start.3 = ((bf16[64,160,128]{2,1,0:T(8,128)(2,1)}), bf16[64,160,128]{2,1,0:T(8,128)(2,1)S(1)}, u32[]{:S(2)}, u32[]{:S(2)}) async-start(bf16[64,160,128]{2,1,0:T(8,128)(2,1)} %reshape.134), calls=%async_computation.3 | async-start | bytes 5242880 | tf_op jit(solution)/shard_map/all_to_all | solution.py:47
  172.0 6.6 %copy-start.1 = (bf16[64,4096]{1,0:T(8,128)(2,1)S(1)}, bf16[64,4096]{1,0:T(8,128)(2,1)}, u32[]{:S(2)}) copy-start(bf16[64,4096]{1,0:T(8,128)(2,1)} %param.6) | copy-start | bytes 1572868

commit v2 on v1

v2 whole, which is shorter than its diff:
```python
import functools

import jax
import jax.numpy as jnp
from jax import lax
from jax.experimental import pallas as pl
from jax.experimental.pallas import tpu as pltpu
from jax.sharding import PartitionSpec as P

LANES = 128
ROW_BLOCK = 64
FF_BLOCK = 256
COLUMN_BLOCK = 2048
STAGGER = 530
VMEM_LIMIT = 60 * 1024 * 1024


def dispatch_kernel(capacity, late_ref, ids_ref, tokens_ref, out_ref, place_ref,
                    rows_ref, spin_ref, where_ref, sem):
    top_count, tok_count = ids_ref.shape
    experts_count = out_ref.shape[0] // capacity
    parts = out_ref.shape[1]
    ids = ids_ref[...]
    name = lax.broadcasted_iota(jnp.int32, (experts_count, tok_count), 0)
    chosen = jnp.zeros((experts_count, tok_count), jnp.float32)
    for k in range(top_count):
        chosen += (ids[k:k + 1] == name).astype(jnp.float32)
    earlier = (lax.broadcasted_iota(jnp.int32, (tok_count, tok_count), 0)
               < lax.broadcasted_iota(jnp.int32, (tok_count, tok_count), 1))
    rank = jnp.dot(chosen.astype(jnp.bfloat16),
                   earlier.astype(jnp.float32).astype(jnp.bfloat16),
                   preferred_element_type=jnp.float32)
    start = rank + (name * capacity).astype(jnp.float32)
    place_ref[...] = jnp.zeros_like(place_ref)
    for k in range(top_count):
        place = jnp.sum(jnp.where(ids[k:k + 1] == name, start, 0.0), axis=0, keepdims=True)
        place_ref[k:k + 1, :tok_count] = place.astype(jnp.int32)
    copy = pltpu.make_async_copy(place_ref, where_ref, sem)
    copy.start()
    for part in range(parts):
        rows_ref[pl.ds(part, tok_count, stride=parts), :] = (
            tokens_ref[:, part * LANES:(part + 1) * LANES].astype(jnp.float32))
    spin_ref[...] = lax.fori_loop(
        0, late_ref[0], lambda i, a: jnp.sin(a) * 0.5 + 1.0, jnp.ones((8, LANES), jnp.float32))
    copy.wait()

    @pl.loop(0, tok_count)
    def _(t):
        first = pl.multiple_of(t * parts, parts)
        row = rows_ref[pl.ds(first, parts), :].astype(out_ref.dtype)
        for k in range(top_count):
            out_ref[where_ref[k, t]] = row


def dispatch(late, ids, tokens, experts_count, capacity):
    top_count, tok_count = ids.shape
    parts = tokens.shape[1] // LANES
    vmem = pl.BlockSpec(memory_space=pltpu.VMEM)
    smem = pl.BlockSpec(memory_space=pltpu.SMEM)
    return pl.pallas_call(
        functools.partial(dispatch_kernel, capacity),
        out_shape=(
            jax.ShapeDtypeStruct((experts_count * capacity, parts, LANES), tokens.dtype),
            jax.ShapeDtypeStruct((top_count, LANES), jnp.int32),
        ),
        in_specs=[smem, vmem, vmem],
        out_specs=(vmem, vmem),
        scratch_shapes=[
            pltpu.VMEM((tok_count * parts, LANES), jnp.float32),
            pltpu.VMEM((8, LANES), jnp.float32),
            pltpu.SMEM((top_count, LANES), jnp.int32),
            pltpu.SemaphoreType.DMA,
        ],
        compiler_params=pltpu.CompilerParams(vmem_limit_bytes=VMEM_LIMIT),
        name="dispatch",
    )(late, ids, tokens)


def expert_kernel(ff_steps, came_ref, gate_ref, up_ref, down_ref, out_ref,
                  wide_ref, rows_ref, hidden_ref, result_ref):
    step = pl.program_id(0)
    count, parts = came_ref.shape[0], came_ref.shape[1]
    out_parts = out_ref.shape[1]

    @pl.when(step == 0)
    def _():
        @pl.loop(0, count // ROW_BLOCK)
        def _(b):
            at = pl.multiple_of(b * ROW_BLOCK, ROW_BLOCK)
            block = came_ref[pl.ds(at, ROW_BLOCK)].astype(jnp.float32)
            wide_ref[...] = block.reshape(ROW_BLOCK * parts, LANES)
            for part in range(parts):
                rows_ref[pl.ds(at, ROW_BLOCK), part * LANES:(part + 1) * LANES] = (
                    wide_ref[pl.ds(part, ROW_BLOCK, stride=parts), :].astype(rows_ref.dtype))

    @pl.when(step < ff_steps)
    def _():
        contract = (((1,), (1,)), ((), ()))
        rows = rows_ref[...]
        gate = lax.dot_general(rows, gate_ref[...], contract, preferred_element_type=jnp.float32)
        up = lax.dot_general(rows, up_ref[...], contract, preferred_element_type=jnp.float32)
        hidden = gate / (1.0 + jnp.exp(-gate)) * up
        at = pl.multiple_of(step * FF_BLOCK, FF_BLOCK)
        hidden_ref[:, pl.ds(at, FF_BLOCK)] = hidden.astype(hidden_ref.dtype)

    @pl.when(step >= ff_steps)
    def _():
        hidden = hidden_ref[...]
        for piece in range(COLUMN_BLOCK // 256):
            result = jnp.dot(hidden, down_ref[:, piece * 256:(piece + 1) * 256],
                             preferred_element_type=jnp.float32)
            for half in range(2):
                result_ref[pl.ds(2 * piece + half, count, stride=out_parts), :] = (
                    result[:, half * LANES:(half + 1) * LANES])

        @pl.loop(0, count // ROW_BLOCK)
        def _(b):
            at = pl.multiple_of(b * ROW_BLOCK, ROW_BLOCK)
            first = pl.multiple_of(b * ROW_BLOCK * out_parts, ROW_BLOCK * out_parts)
            block = result_ref[pl.ds(first, ROW_BLOCK * out_parts), :]
            out_ref[pl.ds(at, ROW_BLOCK)] = block.reshape(
                ROW_BLOCK, out_parts, LANES).astype(out_ref.dtype)


def expert(came, gate, up, down):
    count, parts, _ = came.shape
    ff, width = gate.shape
    ff_steps, column_steps = ff // FF_BLOCK, width // COLUMN_BLOCK
    out_parts = COLUMN_BLOCK // LANES
    return pl.pallas_call(
        functools.partial(expert_kernel, ff_steps),
        out_shape=jax.ShapeDtypeStruct(came.shape, came.dtype),
        grid=(ff_steps + column_steps,),
        in_specs=[
            pl.BlockSpec((count, parts, LANES), lambda i: (0, 0, 0),
                         pipeline_mode=pl.Buffered(1)),
            pl.BlockSpec((FF_BLOCK, width), lambda i: (jnp.minimum(i, ff_steps - 1), 0)),
            pl.BlockSpec((FF_BLOCK, width), lambda i: (jnp.minimum(i, ff_steps - 1), 0)),
            pl.BlockSpec((ff, COLUMN_BLOCK), lambda i: (0, jnp.maximum(i - ff_steps, 0))),
        ],
        out_specs=pl.BlockSpec((count, out_parts, LANES),
                               lambda i: (0, jnp.maximum(i - ff_steps, 0), 0)),
        scratch_shapes=[
            pltpu.VMEM((ROW_BLOCK * parts, LANES), jnp.float32),
            pltpu.VMEM((count, width), came.dtype),
            pltpu.VMEM((count, ff), came.dtype),
            pltpu.VMEM((count * out_parts, LANES), jnp.float32),
        ],
        compiler_params=pltpu.CompilerParams(vmem_limit_bytes=VMEM_LIMIT),
        cost_estimate=pl.CostEstimate(
            flops=6 * count * ff * width, transcendentals=count * ff,
            bytes_accessed=2 * (3 * ff * width + 2 * count * width)),
        name="expert",
    )(came, gate, up, down)


def combine_kernel(place_ref, share_ref, back_ref, out_ref, total_ref):
    top_count, tok_count = share_ref.shape
    parts = back_ref.shape[1]

    @pl.loop(0, tok_count)
    def _(t):
        total = jnp.zeros((parts, LANES), jnp.float32)
        for k in range(top_count):
            total += share_ref[k, t] * back_ref[place_ref[k, t]].astype(jnp.float32)
        total_ref[pl.ds(pl.multiple_of(t * parts, parts), parts), :] = total

    for part in range(parts):
        out_ref[:, part * LANES:(part + 1) * LANES] = (
            total_ref[pl.ds(part, tok_count, stride=parts), :].astype(out_ref.dtype))


def combine(place, share, back):
    tok_count = share.shape[1]
    count, parts, _ = back.shape
    step_parts = parts // 2
    smem = pl.BlockSpec(memory_space=pltpu.SMEM)
    return pl.pallas_call(
        combine_kernel,
        out_shape=jax.ShapeDtypeStruct((tok_count, parts * LANES), back.dtype),
        grid=(2,),
        in_specs=[smem, smem,
                  pl.BlockSpec((count, step_parts, LANES), lambda i: (0, i, 0))],
        out_specs=pl.BlockSpec((tok_count, step_parts * LANES), lambda i: (0, i)),
        scratch_shapes=[pltpu.VMEM((tok_count * step_parts, LANES), jnp.float32)],
        compiler_params=pltpu.CompilerParams(vmem_limit_bytes=VMEM_LIMIT),
        name="combine",
    )(place, share, back)


def swap_join(part, axis):
    other = lax.ppermute(part, "fsdp", [(0, 1), (1, 0)])
    first = lax.axis_index("fsdp") == 0
    return jnp.concatenate(
        [jnp.where(first, part, other), jnp.where(first, other, part)], axis=axis)


def exchange(rows, experts_count):
    sent = rows.reshape(experts_count, -1, LANES)
    came = lax.all_to_all(sent, "expert", split_axis=0, concat_axis=0, tiled=True)
    return came.reshape(rows.shape)


def body(tokens, expert_ids, route_weight, gate_weight, up_weight, down_weight):
    experts_count = lax.axis_size("expert") * gate_weight.shape[0]
    tok_count, top_count = expert_ids.shape
    capacity = tok_count * top_count // experts_count + 1
    late = (lax.axis_index("fsdp") * STAGGER).astype(jnp.int32).reshape(1)
    sent, place = dispatch(late, expert_ids.T, tokens, experts_count, capacity)
    came = exchange(sent, experts_count)
    gate_full = swap_join(gate_weight[0], 0)
    up_full = swap_join(up_weight[0], 0)
    down_full = swap_join(down_weight[0], 1)
    back = exchange(expert(came, gate_full, up_full, down_full), experts_count)
    return combine(place, route_weight.T, back)


def solution(mesh):
    placed = (
        P(("fsdp", "expert"), None),
        P(("fsdp", "expert"), None),
        P(("fsdp", "expert"), None),
        P("expert", "fsdp", None),
        P("expert", "fsdp", None),
        P("expert", None, "fsdp"),
    )
    return jax.shard_map(
        body, mesh=mesh, in_specs=placed, out_specs=P(("fsdp", "expert"), None), check_vma=False
    )
```

time: 181 us -> 182 us (level); the launches traced: 179 us -> 182 us
  blocking collectives: 0 us -> 67.6 us
  matrix products: 41.5 us -> 0 us
  Pallas kernels: 0 us -> 41.2 us
  local copies, waits for them, and re-layouts: 33.5 us -> 1.66 us
  starting transfers between devices: 40 us -> 13 us
  waiting for transfers between devices: 49.4 us -> 39.5 us
  other arithmetic: 13.9 us -> 18.6 us
    all_to_all x0 -> x1, blocking collectives: none -> 67.6 us  [exchange(): lax.all_to_all(sent, 'expert', split_axis=0, concat_axis=0, tiled=True)]
    dot_general x9 -> x0, matrix products: 41.5 us -> none  [the longest x2 23.5 us: expert(): jnp.dot(hidden, down_full, preferred_element_type=jnp.float32)]
    pallas_call x0 -> x3, Pallas kernels: none -> 41.2 us  [the longest x1 27.5 us: expert(): pl.pallas_call(functools.partial(expert_kernel, ff_steps), out_shape=jax....]
    reshape x8 -> x0, local copies, waits for them, and re-layouts: 29.7 us -> none  [the longest x4 15.1 us: exchange(): sent = rows.reshape(experts_count, count * width // LANES, LANES)]
    all_to_all x4 -> x1, starting transfers between devices: 37.8 us -> 11.5 us  [exchange(): lax.all_to_all(sent, 'expert', split_axis=0, concat_axis=0, tiled=True)]
    concatenate x0 -> x3, other arithmetic: none -> 10.3 us  [swap_join(): jnp.concatenate([jnp.where(first, part, other), jnp.where(first, other, p...]
    all_to_all x4 -> x1, waiting for transfers between devices: 49.4 us -> 39.5 us  [exchange(): lax.all_to_all(sent, 'expert', split_axis=0, concat_axis=0, tiled=True)]
    select_n x3 -> x2, other arithmetic: 13.4 us -> 8.32 us  [swap_join(): jnp.where(first, part, other)]
  transfers between devices with their start and end apart: 7 -> 4, of which waited for: 3 -> 1; matrix products, arithmetic and copies ran while one was open for 45% -> 10% of each run, Pallas kernels for 0% -> 5%
where the time goes in v2:
time: 182 us
  blocking collectives  67.6 us (37%)
  Pallas kernels  41.2 us (23%)
  waiting for transfers between devices  39.5 us (22%)
  other arithmetic  18.6 us (10%)
  starting transfers between devices  13 us (7%)
    all_to_all x1, blocking collectives, exchange(): lax.all_to_all(sent, 'expert', split_axis=0, concat_axis=0, tiled=True)  67.6 us
    all_to_all x1, waiting for transfers between devices, exchange(): lax.all_to_all(sent, 'expert', split_axis=0, concat_axis=0, tiled=True)  39.5 us
    pallas_call x1, Pallas kernels, expert(): pl.pallas_call(functools.partial(expert_kernel, ff_steps), out_shape=jax....  27.5 us
    all_to_all x1, starting transfers between devices, exchange(): lax.all_to_all(sent, 'expert', split_axis=0, concat_axis=0, tiled=True)  11.5 us
    concatenate x3, other arithmetic, swap_join(): jnp.concatenate([jnp.where(first, part, other), jnp.where(first, other, p...  10.3 us
    select_n x2, other arithmetic, swap_join(): jnp.where(first, part, other)  8.32 us
    pallas_call x1, Pallas kernels, dispatch(): pl.pallas_call(functools.partial(dispatch_kernel, capacity), out_shape=(j...  8.28 us
    pallas_call x1, Pallas kernels, combine(): pl.pallas_call(combine_kernel, out_shape=jax.ShapeDtypeStruct((tok_count,...  5.39 us
  transfers between devices with their start and end apart: 4, of which 1 were waited for; matrix products, arithmetic and copies ran while one was open for 10% of the time, Pallas kernels for 5%

profile of v2, /device:TPU:1, one launch (start us, length us, event | category | flops | bytes accessed | tf_op | source)
XLA Modules:
  0.0 181.6 jit_solution(10076655154524115631)
XLA Ops:
  0.0 1.4 collective-permute-start
  1.4 0.0 collective-permute-start.1
  1.4 8.3 %dispatch.1 = (bf16[576,32,128]{2,1,0:T(8,128)(2,1)}, s32[8,128]{1,0:T(8,128)}) custom-call(s32[1]{0:T(128)} %bitcast.late_ref, s32[8,64]{1,0:T(8,128)} %bitcast.21, bf16[64,4096]{1,0:T(8,128)(2,1)} %tokens_ref.1), custom_call_target="tpu_custom_call" | custom-call | tf_op jit(solution)/shard_map/dispatch/pallas_call | solution.py:60
  9.7 11.5 %all-to-all-start = ((bf16[64,288,128]{2,1,0:T(8,128)(2,1)}), bf16[64,288,128]{2,1,0:T(8,128)(2,1)}, u32[]{:S(2)}, u32[]{:S(2)}) async-start(bf16[64,288,128]{2,1,0:T(8,128)(2,1)} %bitcast.17), calls=%async_computation | async-start | bytes 9437184 | tf_op jit(solution)/shard_map/all_to_all | solution.py:200
  21.2 0.1 collective-permute-start.2
  21.3 0.0 collective-permute-done
  21.3 0.0 copy-start
  21.3 1.7 copy-done
  23.0 0.0 collective-permute-done.1
  23.0 5.1 %broadcast_select_fusion.3 = (bf16[384,4096]{1,0:T(8,128)(2,1)S(1)}, bf16[384,4096]{1,0:T(8,128)(2,1)S(1)}, bf16[384,4096]{1,0:T(8,128)(2,1)S(1)}, bf16[384,4096]{1,0:T(8,128)(2,1)S(1)}) fusion(bf16[384,4096]{1,0:T(8,128)(2,1)} %collective-permute-done.1, pred[]{:T(512)S(6)} %eq.2, bf16[1,384,4096]{2,1,0:T(8,128)(2,1)} %param.10, ...), kind=kLoop, calls=%fused_computation.6 | loop fusion | flops 6291456 | bytes 25165824 | tf_op jit(solution)/shard_map/jit(_where)/select_n | solution.py:195
  28.0 3.4 %pad_maximum_fusion.1.up_ref = bf16[768,4096]{1,0:T(8,128)(2,1)} fusion(bf16[384,4096]{1,0:T(8,128)(2,1)S(1)} %get-tuple-element.12, bf16[384,4096]{1,0:T(8,128)(2,1)S(1)} %get-tuple-element.11), kind=kLoop, calls=%fused_computation.1 | loop fusion | flops 12582912 | bytes 12582912 | tf_op jit(solution)/shard_map/concatenate | solution.py:194
  31.5 3.5 %pad_maximum_fusion.gate_ref = bf16[768,4096]{1,0:T(8,128)(2,1)} fusion(bf16[384,4096]{1,0:T(8,128)(2,1)S(1)} %get-tuple-element.15, bf16[384,4096]{1,0:T(8,128)(2,1)S(1)} %get-tuple-element.16), kind=kLoop, calls=%fused_computation | loop fusion | flops 12582912 | bytes 12582912 | tf_op jit(solution)/shard_map/concatenate | solution.py:194
  34.9 0.0 collective-permute-done.2
  34.9 3.3 %broadcast_select_fusion.1 = (bf16[768,2048]{1,0:T(8,128)(2,1)S(1)}, bf16[768,2048]{1,0:T(8,128)(2,1)S(1)}) fusion(bf16[768,2048]{1,0:T(8,128)(2,1)} %collective-permute-done.2, pred[]{:T(512)S(6)} %eq.2, bf16[1,768,2048]{2,1,0:T(8,128)(2,1)} %param.11), kind=kLoop, calls=%fused_computation.4 | loop fusion | flops 3145728 | bytes 12582913 | tf_op jit(solution)/shard_map/jit(_where)/select_n | solution.py:195
  38.2 3.4 %pad_maximum_fusion.2.down_ref = bf16[768,4096]{1,0:T(8,128)(2,1)} fusion(bf16[768,2048]{1,0:T(8,128)(2,1)S(1)} %get-tuple-element.10, bf16[768,2048]{1,0:T(8,128)(2,1)S(1)} %get-tuple-element.9), kind=kLoop, calls=%fused_computation.2 | loop fusion | flops 12582912 | bytes 12582912 | tf_op jit(solution)/shard_map/concatenate | solution.py:194
  41.6 39.5 %all-to-all-done = bf16[64,288,128]{2,1,0:T(8,128)(2,1)} async-done(((bf16[64,288,128]{2,1,0:T(8,128)(2,1)}), bf16[64,288,128]{2,1,0:T(8,128)(2,1)}, u32[]{:S(2)}, u32[]{:S(2)}) %all-to-all-start) | async-done | bytes 4718624 | tf_op jit(solution)/shard_map/all_to_all | solution.py:200
  81.1 27.5 %expert.1 = bf16[576,32,128]{2,1,0:T(8,128)(2,1)} custom-call(bf16[576,32,128]{2,1,0:T(8,128)(2,1)} %bitcast.4.came_ref, bf16[768,4096]{1,0:T(8,128)(2,1)} %pad_maximum_fusion.gate_ref, bf16[768,4096]{1,0:T(8,128)(2,1)} %pad_maximum_fusion.1.up_ref, bf16[768,4096]{1,0:T(8,128)(2,1)} %pad_maximum_fusion.2.down_ref), custom_call_target="tpu_custom_call" | custom-call | flops 10871635968 | bytes 28311552 | tf_op jit(solution)/shard_map/expert/pallas_call | solution.py:130
  108.6 67.6 %all_to_all.10 = bf16[64,288,128]{2,1,0:T(8,128)(2,1)} all-to-all(bf16[64,288,128]{2,1,0:T(8,128)(2,1)} %bitcast.18), channel_id=1, replica_groups=mesh['fsdp'=2,'expert'=64] {'expert'}, dimensions={0} | all-to-all | bytes 9437184 | tf_op jit(solution)/shard_map/all_to_all | solution.py:200
  176.2 5.4 %combine.1 = bf16[64,4096]{1,0:T(8,128)(2,1)} custom-call(s32[8,128]{1,0:T(8,128)} %get-tuple-element.7.place_ref, f32[8,64]{1,0:T(8,128)} %bitcast.22, bf16[576,32,128]{2,1,0:T(8,128)(2,1)} %bitcast.16), custom_call_target="tpu_custom_call" | custom-call | tf_op jit(solution)/shard_map/combine/pallas_call | solution.py:178
Async XLA Ops:
  0.0 21.3 %collective-permute-start = (bf16[384,4096]{1,0:T(8,128)(2,1)}, bf16[384,4096]{1,0:T(8,128)(2,1)S(1)}, u32[]{:S(2)}, u32[]{:S(2)}) collective-permute-start(bf16[384,4096]{1,0:T(8,128)(2,1)} %bitcast.20), channel_id=1, source_target_pairs={{0,64},{64,0},{1,65},{65,1},{2,66},{66,2},{3,67},{67,3},{4,68},{68... | collective-permute-start | bytes 9437192 | tf_op jit(solution)/shard_map/ppermute | solution.py:192
  1.4 21.5 %collective-permute-start.1 = (bf16[384,4096]{1,0:T(8,128)(2,1)}, bf16[384,4096]{1,0:T(8,128)(2,1)}, u32[]{:S(2)}, u32[]{:S(2)}) collective-permute-start(bf16[384,4096]{1,0:T(8,128)(2,1)} %bitcast.19), channel_id=1, source_target_pairs={{0,64},{64,0},{1,65},{65,1},{2,66},{66,2},{3,67},{67,3},{4,68},{68... | collective-permute-start | bytes 9437192 | tf_op jit(solution)/shard_map/ppermute | solution.py:192
  9.7 71.4 %all-to-all-start = ((bf16[64,288,128]{2,1,0:T(8,128)(2,1)}), bf16[64,288,128]{2,1,0:T(8,128)(2,1)}, u32[]{:S(2)}, u32[]{:S(2)}) async-start(bf16[64,288,128]{2,1,0:T(8,128)(2,1)} %bitcast.17), calls=%async_computation | async-start | bytes 9437184 | tf_op jit(solution)/shard_map/all_to_all | solution.py:200
  21.2 13.8 %collective-permute-start.2 = (bf16[768,2048]{1,0:T(8,128)(2,1)}, bf16[768,2048]{1,0:T(8,128)(2,1)}, u32[]{:S(2)}, u32[]{:S(2)}) collective-permute-start(bf16[768,2048]{1,0:T(8,128)(2,1)} %bitcast.7), channel_id=1, source_target_pairs={{0,64},{64,0},{1,65},{65,1},{2,66},{66,2},{3,67},{67,3},{4,68},{68... | collective-permute-start | bytes 9437192 | tf_op jit(solution)/shard_map/ppermute | solution.py:192
  21.3 1.7 copy-start

commit v3 on v2

v3 whole, which is shorter than its diff:
```python
import functools

import jax
import jax.numpy as jnp
from jax import lax
from jax.experimental import pallas as pl
from jax.experimental.pallas import tpu as pltpu
from jax.sharding import PartitionSpec as P

LANES = 128
ROW_BLOCK = 64
FF_BLOCK = 128
COLUMN_BLOCK = 2048
STAGGER = 530
EXPERT_GROUP = 8
DISPATCH_LIMIT = 60 * 1024 * 1024
SMALL_LIMIT = 14 * 1024 * 1024
EXPERT_LIMIT = 48 * 1024 * 1024


def padded(parts):
    return parts + 8


def dispatch_kernel(capacity, late_ref, ids_ref, tokens_ref, out_ref, place_ref,
                    wide_ref, rows_ref, stage_ref, table_ref, where_ref, table_sem, out_sem):
    top_count, tok_count = ids_ref.shape
    parts = rows_ref.shape[1]
    experts_count = out_ref.shape[0] // capacity
    pitch = padded(parts)
    ids = ids_ref[...]
    name = lax.broadcasted_iota(jnp.int32, (experts_count, tok_count), 0)
    token = lax.broadcasted_iota(jnp.int32, (experts_count, tok_count), 1)
    chosen = jnp.zeros((experts_count, tok_count), jnp.float32)
    for k in range(top_count):
        chosen += (ids[k:k + 1] == name).astype(jnp.float32)
    earlier = (lax.broadcasted_iota(jnp.int32, (tok_count, tok_count), 0)
               < lax.broadcasted_iota(jnp.int32, (tok_count, tok_count), 1))
    rank = jnp.dot(chosen.astype(jnp.bfloat16),
                   earlier.astype(jnp.float32).astype(jnp.bfloat16),
                   preferred_element_type=jnp.float32)
    held = jnp.where(chosen > 0.0, rank, -1.0)
    lane = lax.broadcasted_iota(jnp.int32, (experts_count, LANES), 1)
    table = jnp.zeros((experts_count, LANES), jnp.float32)
    for slot in range(capacity):
        source = jnp.sum(jnp.where(held == float(slot), token.astype(jnp.float32), 0.0),
                         axis=1, keepdims=True)
        table = jnp.where(lane == slot, source, table)
    table_ref[...] = table.astype(jnp.int32)
    copy = pltpu.make_async_copy(table_ref, where_ref, table_sem)
    copy.start()
    place_ref[...] = lax.fori_loop(
        0, late_ref[0], lambda i, a: jnp.sin(a) * 0.5 + 1.0,
        jnp.ones(place_ref.shape, jnp.float32)).astype(jnp.int32)
    start = rank + (name * capacity).astype(jnp.float32)
    for k in range(top_count):
        place = jnp.sum(jnp.where(ids[k:k + 1] == name, start, 0.0), axis=0, keepdims=True)
        place_ref[k:k + 1, :tok_count] = place.astype(jnp.int32)
    for part in range(parts):
        wide_ref[pl.ds(part, tok_count, stride=pitch), :] = (
            tokens_ref[:, part * LANES:(part + 1) * LANES].astype(jnp.float32))
    for t in range(tok_count):
        rows_ref[t] = wide_ref[t * pitch:t * pitch + parts, :].astype(rows_ref.dtype)
    copy.wait()

    group = EXPERT_GROUP * capacity

    def send(g):
        at = pl.multiple_of(g * group, group)
        return pltpu.make_async_copy(stage_ref.at[pl.ds(at, group)],
                                     out_ref.at[pl.ds(at, group)], out_sem.at[g])

    @pl.loop(0, experts_count // EXPERT_GROUP)
    def _(g):
        @pl.loop(0, EXPERT_GROUP)
        def _(i):
            e = g * EXPERT_GROUP + i
            for slot in range(capacity):
                stage_ref[e * capacity + slot] = rows_ref[where_ref[e, slot]]
        send(g).start()

    @pl.loop(0, experts_count // EXPERT_GROUP)
    def _(g):
        send(g).wait()


def dispatch(late, ids, tokens, experts_count, capacity):
    top_count, tok_count = ids.shape
    parts = tokens.shape[1] // LANES
    count = experts_count * capacity
    vmem = pl.BlockSpec(memory_space=pltpu.VMEM)
    smem = pl.BlockSpec(memory_space=pltpu.SMEM)
    return pl.pallas_call(
        functools.partial(dispatch_kernel, capacity),
        out_shape=(
            jax.ShapeDtypeStruct((count, parts, LANES), tokens.dtype),
            jax.ShapeDtypeStruct((top_count, LANES), jnp.int32),
        ),
        in_specs=[smem, vmem, vmem],
        out_specs=(pl.BlockSpec(memory_space=pltpu.HBM), vmem),
        scratch_shapes=[
            pltpu.VMEM((tok_count * padded(parts), LANES), jnp.float32),
            pltpu.VMEM((tok_count, parts, LANES), tokens.dtype),
            pltpu.VMEM((count, parts, LANES), tokens.dtype),
            pltpu.VMEM((experts_count, LANES), jnp.int32),
            pltpu.SMEM((experts_count, LANES), jnp.int32),
            pltpu.SemaphoreType.DMA,
            pltpu.SemaphoreType.DMA((experts_count // EXPERT_GROUP,)),
        ],
        compiler_params=pltpu.CompilerParams(vmem_limit_bytes=DISPATCH_LIMIT),
        name="dispatch",
    )(late, ids, tokens)


def settle_kernel(gate_ref, up_ref, down_ref, gate_out_ref, up_out_ref, down_out_ref):
    del gate_ref, up_ref, down_ref, gate_out_ref, up_out_ref, down_out_ref


def partner_weights(parts):
    others = [lax.ppermute(part, "fsdp", [(0, 1), (1, 0)]) for part in parts]
    hbm = pl.BlockSpec(memory_space=pltpu.HBM)
    return pl.pallas_call(
        settle_kernel,
        out_shape=tuple(jax.ShapeDtypeStruct(part.shape, part.dtype) for part in others),
        in_specs=[hbm] * 3,
        out_specs=(hbm,) * 3,
        input_output_aliases={0: 0, 1: 1, 2: 2},
        cost_estimate=pl.CostEstimate(
            flops=10**11, transcendentals=0, bytes_accessed=4 * 10**8),
        name="settle",
    )(*others)


def expert_kernel(came_ref, gate_ref, up_ref, down_ref, gate_other_ref, up_other_ref,
                  down_other_ref, out_ref, held_ref, gate_all_ref, up_all_ref, down_all_ref,
                  wide_ref, rows_ref, hidden_ref, result_ref, came_sem, gate_sem, up_sem,
                  down_sem):
    count, parts = came_ref.shape[0], came_ref.shape[1]
    half_ff, width = gate_ref.shape
    columns = down_ref.shape[1]
    pitch = padded(parts)
    mine = lax.axis_index("fsdp")

    def fetch(b):
        at = pl.multiple_of(b * ROW_BLOCK, ROW_BLOCK)
        return pltpu.make_async_copy(came_ref.at[pl.ds(at, ROW_BLOCK)],
                                     held_ref.at[pl.ds(at, ROW_BLOCK)], came_sem.at[b])

    @pl.loop(0, count // ROW_BLOCK)
    def _(b):
        fetch(b).start()

    gate_copies, up_copies = [], []
    for low in range(0, 2 * half_ff, FF_BLOCK):
        own = low < half_ff
        at = low % half_ff
        step = low // FF_BLOCK
        gate_copies.append(pltpu.make_async_copy(
            (gate_ref if own else gate_other_ref).at[at:at + FF_BLOCK],
            gate_all_ref.at[low:low + FF_BLOCK], gate_sem.at[step]))
        up_copies.append(pltpu.make_async_copy(
            (up_ref if own else up_other_ref).at[at:at + FF_BLOCK],
            up_all_ref.at[low:low + FF_BLOCK], up_sem.at[step]))
        gate_copies[-1].start()
        up_copies[-1].start()
    down_copies = []
    for which, (part, index) in enumerate(((down_ref, mine), (down_other_ref, 1 - mine))):
        to = pl.multiple_of(index * columns, columns)
        for half, owner in enumerate((mine, 1 - mine)):
            at = pl.multiple_of(owner * half_ff, half_ff)
            down_copies.append(pltpu.make_async_copy(
                part.at[pl.ds(at, half_ff)],
                down_all_ref.at[half * half_ff:(half + 1) * half_ff, pl.ds(to, columns)],
                down_sem.at[2 * which + half]))
            down_copies[-1].start()

    @pl.loop(0, count // ROW_BLOCK)
    def _(b):
        fetch(b).wait()
        at = pl.multiple_of(b * ROW_BLOCK, ROW_BLOCK)
        for row in range(ROW_BLOCK):
            wide_ref[row * pitch:row * pitch + parts, :] = held_ref[at + row].astype(jnp.float32)
        for part in range(parts):
            rows_ref[pl.ds(at, ROW_BLOCK), part * LANES:(part + 1) * LANES] = (
                wide_ref[pl.ds(part, ROW_BLOCK, stride=pitch), :].astype(rows_ref.dtype))

    contract = (((1,), (1,)), ((), ()))
    for step, low in enumerate(range(0, 2 * half_ff, FF_BLOCK)):
        gate_copies[step].wait()
        up_copies[step].wait()
        rows = rows_ref[...]
        gate = lax.dot_general(rows, gate_all_ref[low:low + FF_BLOCK], contract,
                               preferred_element_type=jnp.float32)
        up = lax.dot_general(rows, up_all_ref[low:low + FF_BLOCK], contract,
                             preferred_element_type=jnp.float32)
        hidden = gate / (1.0 + jnp.exp(-gate)) * up
        hidden_ref[:, low:low + FF_BLOCK] = hidden.astype(hidden_ref.dtype)
    for copy in down_copies:
        copy.wait()

    out_parts = COLUMN_BLOCK // LANES
    out_pitch = padded(out_parts)
    for block in range(width // COLUMN_BLOCK):
        for piece in range(COLUMN_BLOCK // 256):
            low = block * COLUMN_BLOCK + piece * 256
            result = jnp.dot(hidden_ref[...], down_all_ref[:, low:low + 256],
                             preferred_element_type=jnp.float32)
            for half in range(2):
                result_ref[pl.ds(2 * piece + half, count, stride=out_pitch), :] = (
                    result[:, half * LANES:(half + 1) * LANES])

        @pl.loop(0, count // ROW_BLOCK)
        def _(b):
            at = pl.multiple_of(b * ROW_BLOCK, ROW_BLOCK)
            for row in range(ROW_BLOCK):
                first = pl.multiple_of((at + row) * out_pitch, 8)
                out_ref[at + row, block * out_parts:(block + 1) * out_parts] = (
                    result_ref[pl.ds(first, out_parts), :].astype(out_ref.dtype))


def expert(came, own, other):
    count, parts, _ = came.shape
    half_ff, width = own[0].shape
    ff, dtype = 2 * half_ff, came.dtype
    steps = ff // FF_BLOCK
    anywhere = pl.BlockSpec(memory_space=pl.ANY)
    return pl.pallas_call(
        expert_kernel,
        out_shape=jax.ShapeDtypeStruct(came.shape, dtype),
        in_specs=[anywhere] * 7,
        out_specs=pl.BlockSpec(memory_space=pltpu.VMEM),
        scratch_shapes=[
            pltpu.VMEM(came.shape, dtype),
            pltpu.VMEM((ff, width), dtype),
            pltpu.VMEM((ff, width), dtype),
            pltpu.VMEM((ff, width), dtype),
            pltpu.VMEM((ROW_BLOCK * padded(parts), LANES), jnp.float32),
            pltpu.VMEM((count, width), dtype),
            pltpu.VMEM((count, ff), dtype),
            pltpu.VMEM((count * padded(COLUMN_BLOCK // LANES), LANES), jnp.float32),
            pltpu.SemaphoreType.DMA((count // ROW_BLOCK,)),
            pltpu.SemaphoreType.DMA((steps,)),
            pltpu.SemaphoreType.DMA((steps,)),
            pltpu.SemaphoreType.DMA((4,)),
        ],
        compiler_params=pltpu.CompilerParams(vmem_limit_bytes=EXPERT_LIMIT),
        cost_estimate=pl.CostEstimate(
            flops=6 * count * ff * width, transcendentals=count * ff,
            bytes_accessed=2 * (3 * ff * width + 2 * count * width)),
        name="expert",
    )(came, *own, *other)


def combine_kernel(place_ref, share_ref, back_ref, out_ref, total_ref):
    top_count, tok_count = share_ref.shape
    parts = back_ref.shape[1]
    pitch = padded(parts)

    @pl.loop(0, tok_count)
    def _(t):
        total = jnp.zeros((parts, LANES), jnp.float32)
        for k in range(top_count):
            total += share_ref[k, t] * back_ref[place_ref[k, t]].astype(jnp.float32)
        total_ref[pl.ds(pl.multiple_of(t * pitch, 8), parts), :] = total

    for part in range(parts):
        out_ref[:, part * LANES:(part + 1) * LANES] = (
            total_ref[pl.ds(part, tok_count, stride=pitch), :].astype(out_ref.dtype))


def combine(place, share, back):
    tok_count = share.shape[1]
    parts = back.shape[1]
    smem = pl.BlockSpec(memory_space=pltpu.SMEM)
    vmem = pl.BlockSpec(memory_space=pltpu.VMEM)
    return pl.pallas_call(
        combine_kernel,
        out_shape=jax.ShapeDtypeStruct((tok_count, parts * LANES), back.dtype),
        in_specs=[smem, smem, vmem],
        out_specs=vmem,
        scratch_shapes=[pltpu.VMEM((tok_count * padded(parts), LANES), jnp.float32)],
        compiler_params=pltpu.CompilerParams(vmem_limit_bytes=SMALL_LIMIT),
        name="combine",
    )(place, share, back)


def exchange(rows, experts_count):
    sent = rows.reshape(experts_count, -1, LANES)
    came = lax.all_to_all(sent, "expert", split_axis=0, concat_axis=0, tiled=True)
    return came.reshape(rows.shape)


def body(tokens, expert_ids, route_weight, gate_weight, up_weight, down_weight):
    experts_count = lax.axis_size("expert") * gate_weight.shape[0]
    tok_count, top_count = expert_ids.shape
    capacity = tok_count * top_count // experts_count + 1
    late = (lax.axis_index("fsdp") * STAGGER).astype(jnp.int32).reshape(1)
    sent, place = dispatch(late, expert_ids.T, tokens, experts_count, capacity)
    came = exchange(sent, experts_count)
    own = (gate_weight[0], up_weight[0], down_weight[0])
    back = exchange(expert(came, own, partner_weights(own)), experts_count)
    return combine(place, route_weight.T, back)


def solution(mesh):
    placed = (
        P(("fsdp", "expert"), None),
        P(("fsdp", "expert"), None),
        P(("fsdp", "expert"), None),
        P("expert", "fsdp", None),
        P("expert", "fsdp", None),
        P("expert", None, "fsdp"),
    )
    return jax.shard_map(
        body, mesh=mesh, in_specs=placed, out_specs=P(("fsdp", "expert"), None), check_vma=False
    )
```

time: 182 us -> 168 us (0.923)
  other arithmetic: 18.6 us -> 0 us
  Pallas kernels: 41.2 us -> 58.2 us
  blocking collectives: 67.6 us -> 57.9 us
    pallas_call x1, Pallas kernels: 8.28 us -> 28.4 us  [dispatch(): pl.pallas_call(functools.partial(dispatch_kernel, capacity), out_shape=(j...]
    concatenate x3 -> x0, other arithmetic: 10.3 us -> none  [swap_join(): jnp.concatenate([jnp.where(first, part, other), jnp.where(first, other, p...]
    all_to_all x1, blocking collectives: 67.6 us -> 57.9 us  [exchange(): lax.all_to_all(sent, 'expert', split_axis=0, concat_axis=0, tiled=True)]
    select_n x2 -> x0, other arithmetic: 8.32 us -> none  [swap_join(): jnp.where(first, part, other)]
    pallas_call x1, Pallas kernels: 5.39 us -> 3.18 us  [combine(): pl.pallas_call(combine_kernel, out_shape=jax.ShapeDtypeStruct((tok_count,...]
    pallas_call x1 -> x2, Pallas kernels: 27.5 us -> 26.6 us  [the longest x1 26.6 us: expert(): pl.pallas_call(expert_kernel, out_shape=jax.ShapeDtypeStruct(came.shape,...]
  transfers between devices with their start and end apart: 4 -> 4, of which waited for: 1 -> 1; matrix products, arithmetic and copies ran while one was open for 10% -> 0% of each run, Pallas kernels for 5% -> 17%
where the time goes in v3:
time: 168 us
  Pallas kernels  58.2 us (35%)
  blocking collectives  57.9 us (34%)
  waiting for transfers between devices  38 us (23%)
  starting transfers between devices  13.4 us (8%)
    all_to_all x1, blocking collectives, exchange(): lax.all_to_all(sent, 'expert', split_axis=0, concat_axis=0, tiled=True)  57.9 us
    all_to_all x1, waiting for transfers between devices, exchange(): lax.all_to_all(sent, 'expert', split_axis=0, concat_axis=0, tiled=True)  38 us
    pallas_call x1, Pallas kernels, dispatch(): pl.pallas_call(functools.partial(dispatch_kernel, capacity), out_shape=(j...  28.4 us
    pallas_call x1, Pallas kernels, expert(): pl.pallas_call(expert_kernel, out_shape=jax.ShapeDtypeStruct(came.shape,...  26.6 us
    all_to_all x1, starting transfers between devices, exchange(): lax.all_to_all(sent, 'expert', split_axis=0, concat_axis=0, tiled=True)  11.5 us
  transfers between devices with their start and end apart: 4, of which 1 were waited for; matrix products, arithmetic and copies ran while one was open for 0% of the time, Pallas kernels for 17%

profile of v3, /device:TPU:1, one launch (start us, length us, event | category | flops | bytes accessed | tf_op | source)
XLA Modules:
  0.0 167.6 jit_solution(15348128344463867061)
XLA Ops:
  0.0 1.4 collective-permute-start
  1.4 0.0 collective-permute-start.1
  1.4 0.5 collective-permute-start.2
  1.9 28.4 %dispatch.1 = (bf16[576,32,128]{2,1,0:T(8,128)(2,1)}, s32[8,128]{1,0:T(8,128)}) custom-call(s32[1]{0:T(128)} %bitcast.late_ref, s32[8,64]{1,0:T(8,128)} %bitcast.16, bf16[64,4096]{1,0:T(8,128)(2,1)} %tokens_ref.1), custom_call_target="tpu_custom_call" | custom-call | tf_op jit(solution)/shard_map/dispatch/pallas_call | solution.py:93
  30.3 11.5 %all-to-all-start = ((bf16[64,288,128]{2,1,0:T(8,128)(2,1)}), bf16[64,288,128]{2,1,0:T(8,128)(2,1)}, u32[]{:S(2)}, u32[]{:S(2)}) async-start(bf16[64,288,128]{2,1,0:T(8,128)(2,1)} %bitcast.14), calls=%async_computation | async-start | bytes 9437184 | tf_op jit(solution)/shard_map/all_to_all | solution.py:289
  41.8 0.0 copy-start.2
  41.8 0.0 collective-permute-done.gate_ref
  41.8 0.0 collective-permute-done.1.up_ref
  41.8 0.0 collective-permute-done.2.down_ref
  41.8 38.0 %all-to-all-done = bf16[64,288,128]{2,1,0:T(8,128)(2,1)} async-done(((bf16[64,288,128]{2,1,0:T(8,128)(2,1)}), bf16[64,288,128]{2,1,0:T(8,128)(2,1)}, u32[]{:S(2)}, u32[]{:S(2)}) %all-to-all-start) | async-done | bytes 4718624 | tf_op jit(solution)/shard_map/all_to_all | solution.py:289
  79.8 0.0 copy-done.2
  79.8 26.6 %expert.1 = bf16[576,32,128]{2,1,0:T(8,128)(2,1)} custom-call(bf16[576,32,128]{2,1,0:T(8,128)(2,1)} %bitcast.4.came_ref, bf16[384,4096]{1,0:T(8,128)(2,1)S(1)} %bitcast.13, bf16[384,4096]{1,0:T(8,128)(2,1)} %bitcast.18, bf16[768,2048]{1,0:T(8,128)(2,1)} %bitcast.20, bf16[384,4096]{1,0:T(8,128)(2,1)} %get-tuple-element.12.gate_other_ref, ...), custom_call_target="tpu_custom_call" | custom-call | flops 10871635968 | bytes 28311552 | tf_op jit(solution)/shard_map/expert/pallas_call | solution.py:227
  106.4 0.0 copy-start
  106.5 0.0 copy-start.1
  106.5 57.9 %all_to_all.10 = bf16[64,288,128]{2,1,0:T(8,128)(2,1)S(1)} all-to-all(bf16[64,288,128]{2,1,0:T(8,128)(2,1)} %bitcast.15), channel_id=1, replica_groups=mesh['fsdp'=2,'expert'=64] {'expert'}, dimensions={0} | all-to-all | bytes 9437184 | tf_op jit(solution)/shard_map/all_to_all | solution.py:289
  164.4 0.0 copy-done
  164.4 0.0 copy-done.1
  164.4 3.2 %combine.1 = bf16[64,4096]{1,0:T(8,128)(2,1)} custom-call(s32[8,128]{1,0:T(8,128)S(1)} %copy-done.1, f32[8,64]{1,0:T(8,128)S(1)} %bitcast.11, bf16[576,32,128]{2,1,0:T(8,128)(2,1)S(1)} %bitcast.10), custom_call_target="tpu_custom_call" | custom-call | tf_op jit(solution)/shard_map/combine/pallas_call | solution.py:276
  (1 shorter events, 0.0 us)
Async XLA Ops:
  0.0 41.8 %collective-permute-start = (bf16[384,4096]{1,0:T(8,128)(2,1)}, bf16[384,4096]{1,0:T(8,128)(2,1)}, u32[]{:S(2)}, u32[]{:S(2)}) collective-permute-start(bf16[384,4096]{1,0:T(8,128)(2,1)} %bitcast.12), channel_id=1, source_target_pairs={{0,64},{64,0},{1,65},{65,1},{2,66},{66,2},{3,67},{67,3},{4,68},{68... | collective-permute-start | bytes 9437192 | tf_op jit(solution)/shard_map/ppermute | solution.py:120
  1.4 40.4 %collective-permute-start.1 = (bf16[384,4096]{1,0:T(8,128)(2,1)}, bf16[384,4096]{1,0:T(8,128)(2,1)}, u32[]{:S(2)}, u32[]{:S(2)}) collective-permute-start(bf16[384,4096]{1,0:T(8,128)(2,1)} %bitcast.17), channel_id=1, source_target_pairs={{0,64},{64,0},{1,65},{65,1},{2,66},{66,2},{3,67},{67,3},{4,68},{68... | collective-permute-start | bytes 9437192 | tf_op jit(solution)/shard_map/ppermute | solution.py:120
  1.4 40.4 %collective-permute-start.2 = (bf16[768,2048]{1,0:T(8,128)(2,1)}, bf16[768,2048]{1,0:T(8,128)(2,1)}, u32[]{:S(2)}, u32[]{:S(2)}) collective-permute-start(bf16[768,2048]{1,0:T(8,128)(2,1)} %bitcast.19), channel_id=1, source_target_pairs={{0,64},{64,0},{1,65},{65,1},{2,66},{66,2},{3,67},{67,3},{4,68},{68... | collective-permute-start | bytes 9437192 | tf_op jit(solution)/shard_map/ppermute | solution.py:120
  30.3 49.5 %all-to-all-start = ((bf16[64,288,128]{2,1,0:T(8,128)(2,1)}), bf16[64,288,128]{2,1,0:T(8,128)(2,1)}, u32[]{:S(2)}, u32[]{:S(2)}) async-start(bf16[64,288,128]{2,1,0:T(8,128)(2,1)} %bitcast.14), calls=%async_computation | async-start | bytes 9437184 | tf_op jit(solution)/shard_map/all_to_all | solution.py:289
  41.8 38.0 %copy-start.2 = (bf16[1,384,4096]{2,1,0:T(8,128)(2,1)S(1)}, bf16[1,384,4096]{2,1,0:T(8,128)(2,1)}, u32[]{:S(2)}) copy-start(bf16[1,384,4096]{2,1,0:T(8,128)(2,1)} %param.9) | copy-start | bytes 9437188
  106.4 57.9 %copy-start = (f32[64,8]{0,1:T(8,128)S(1)}, f32[64,8]{0,1:T(8,128)}, u32[]{:S(2)}) copy-start(f32[64,8]{0,1:T(8,128)} %param.8) | copy-start | bytes 6148
  106.5 57.9 %copy-start.1 = (s32[8,128]{1,0:T(8,128)S(1)}, s32[8,128]{1,0:T(8,128)}, u32[]{:S(2)}) copy-start(s32[8,128]{1,0:T(8,128)} %get-tuple-element.10.place_ref) | copy-start | bytes 12292

commit v4 on v3

--- a/solution.py
+++ b/solution.py
@@ -9,9 +9,10 @@
 
 LANES = 128
 ROW_BLOCK = 64
-FF_BLOCK = 128
+FF_BLOCK = 256
+PIECE = 128
 COLUMN_BLOCK = 2048
-STAGGER = 530
+STAGGER = 700
 EXPERT_GROUP = 8
 DISPATCH_LIMIT = 60 * 1024 * 1024
 SMALL_LIMIT = 14 * 1024 * 1024
@@ -150,19 +151,16 @@
     def _(b):
         fetch(b).start()
 
-    gate_copies, up_copies = [], []
-    for low in range(0, 2 * half_ff, FF_BLOCK):
-        own = low < half_ff
-        at = low % half_ff
-        step = low // FF_BLOCK
-        gate_copies.append(pltpu.make_async_copy(
-            (gate_ref if own else gate_other_ref).at[at:at + FF_BLOCK],
-            gate_all_ref.at[low:low + FF_BLOCK], gate_sem.at[step]))
-        up_copies.append(pltpu.make_async_copy(
-            (up_ref if own else up_other_ref).at[at:at + FF_BLOCK],
-            up_all_ref.at[low:low + FF_BLOCK], up_sem.at[step]))
-        gate_copies[-1].start()
-        up_copies[-1].start()
+    pairs = ((gate_ref, gate_other_ref, gate_all_ref, gate_sem),
+             (up_ref, up_other_ref, up_all_ref, up_sem))
+    pieces = []
+    for low in range(0, 2 * half_ff, PIECE):
+        at, own = low % half_ff, low < half_ff
+        for first, second, full, sem in pairs:
+            pieces.append(pltpu.make_async_copy(
+                (first if own else second).at[at:at + PIECE],
+                full.at[low:low + PIECE], sem.at[low // PIECE]))
+    per_step = len(pairs) * FF_BLOCK // PIECE
     down_copies = []
     for which, (part, index) in enumerate(((down_ref, mine), (down_other_ref, 1 - mine))):
         to = pl.multiple_of(index * columns, columns)
@@ -172,10 +170,8 @@
                 part.at[pl.ds(at, half_ff)],
                 down_all_ref.at[half * half_ff:(half + 1) * half_ff, pl.ds(to, columns)],
                 down_sem.at[2 * which + half]))
-            down_copies[-1].start()
-
-    @pl.loop(0, count // ROW_BLOCK)
-    def _(b):
+
+    def relay(b):
         fetch(b).wait()
         at = pl.multiple_of(b * ROW_BLOCK, ROW_BLOCK)
         for row in range(ROW_BLOCK):
@@ -184,10 +180,20 @@
             rows_ref[pl.ds(at, ROW_BLOCK), part * LANES:(part + 1) * LANES] = (
                 wide_ref[pl.ds(part, ROW_BLOCK, stride=pitch), :].astype(rows_ref.dtype))
 
+    blocks = count // ROW_BLOCK
+    steps = 2 * half_ff // FF_BLOCK
+    for step in range(steps):
+        for copy in pieces[step * per_step:(step + 1) * per_step]:
+            copy.start()
+        pl.loop(step * blocks // steps, (step + 1) * blocks // steps)(relay)
+    for copy in down_copies:
+        copy.start()
+
     contract = (((1,), (1,)), ((), ()))
-    for step, low in enumerate(range(0, 2 * half_ff, FF_BLOCK)):
-        gate_copies[step].wait()
-        up_copies[step].wait()
+    for step in range(steps):
+        for copy in pieces[step * per_step:(step + 1) * per_step]:
+            copy.wait()
+        low = step * FF_BLOCK
         rows = rows_ref[...]
         gate = lax.dot_general(rows, gate_all_ref[low:low + FF_BLOCK], contract,
                                preferred_element_type=jnp.float32)
@@ -222,7 +228,7 @@
     count, parts, _ = came.shape
     half_ff, width = own[0].shape
     ff, dtype = 2 * half_ff, came.dtype
-    steps = ff // FF_BLOCK
+    steps = ff // PIECE
     anywhere = pl.BlockSpec(memory_space=pl.ANY)
     return pl.pallas_call(
         expert_kernel,

time: 168 us -> 145 us (0.86)
  blocking collectives: 57.9 us -> 39.7 us
  waiting for transfers between devices: 38 us -> 33.3 us
    all_to_all x1, blocking collectives: 57.9 us -> 39.7 us  [exchange(): lax.all_to_all(sent, 'expert', split_axis=0, concat_axis=0, tiled=True)]
    pallas_call x1, Pallas kernels: 26.6 us -> 18.6 us  [expert(): pl.pallas_call(expert_kernel, out_shape=jax.ShapeDtypeStruct(came.shape,...]
    pallas_call x1, Pallas kernels: 28.4 us -> 36 us  [dispatch(): pl.pallas_call(functools.partial(dispatch_kernel, capacity), out_shape=(j...]
    all_to_all x1, waiting for transfers between devices: 38 us -> 33.3 us  [exchange(): lax.all_to_all(sent, 'expert', split_axis=0, concat_axis=0, tiled=True)]
  transfers between devices with their start and end apart: 4 -> 4, of which waited for: 1 -> 1; matrix products, arithmetic and copies ran while one was open for 0% -> 0% of each run, Pallas kernels for 17% -> 25%
where the time goes in v4:
time: 145 us; the launch traced here: 144 us
  Pallas kernels  57.7 us (40%)
  blocking collectives  39.7 us (27%)
  waiting for transfers between devices  33.3 us (23%)
  starting transfers between devices  13.6 us (9%)
    all_to_all x1, blocking collectives, exchange(): lax.all_to_all(sent, 'expert', split_axis=0, concat_axis=0, tiled=True)  39.7 us
    pallas_call x1, Pallas kernels, dispatch(): pl.pallas_call(functools.partial(dispatch_kernel, capacity), out_shape=(j...  36 us
    all_to_all x1, waiting for transfers between devices, exchange(): lax.all_to_all(sent, 'expert', split_axis=0, concat_axis=0, tiled=True)  33.3 us
    pallas_call x1, Pallas kernels, expert(): pl.pallas_call(expert_kernel, out_shape=jax.ShapeDtypeStruct(came.shape,...  18.6 us
    all_to_all x1, starting transfers between devices, exchange(): lax.all_to_all(sent, 'expert', split_axis=0, concat_axis=0, tiled=True)  11.6 us
    pallas_call x1, Pallas kernels, combine(): pl.pallas_call(combine_kernel, out_shape=jax.ShapeDtypeStruct((tok_count,...  3.18 us
  transfers between devices with their start and end apart: 4, of which 1 were waited for; matrix products, arithmetic and copies ran while one was open for 0% of the time, Pallas kernels for 25%

profile of v4, /device:TPU:1, one launch (start us, length us, event | category | flops | bytes accessed | tf_op | source)
XLA Modules:
  0.0 144.4 jit_solution(16281705588835069227)
XLA Ops:
  0.0 1.4 collective-permute-start
  1.4 0.0 collective-permute-start.1
  1.4 0.5 collective-permute-start.2
  1.9 36.0 %dispatch.1 = (bf16[576,32,128]{2,1,0:T(8,128)(2,1)}, s32[8,128]{1,0:T(8,128)}) custom-call(s32[1]{0:T(128)} %bitcast.late_ref, s32[8,64]{1,0:T(8,128)} %bitcast.16, bf16[64,4096]{1,0:T(8,128)(2,1)} %tokens_ref.1), custom_call_target="tpu_custom_call" | custom-call | tf_op jit(solution)/shard_map/dispatch/pallas_call | solution.py:94
  37.9 11.6 %all-to-all-start = ((bf16[64,288,128]{2,1,0:T(8,128)(2,1)}), bf16[64,288,128]{2,1,0:T(8,128)(2,1)}, u32[]{:S(2)}, u32[]{:S(2)}) async-start(bf16[64,288,128]{2,1,0:T(8,128)(2,1)} %bitcast.14), calls=%async_computation | async-start | bytes 9437184 | tf_op jit(solution)/shard_map/all_to_all | solution.py:295
  49.6 0.0 copy-start.2
  49.6 0.0 collective-permute-done.gate_ref
  49.6 0.0 collective-permute-done.1.up_ref
  49.6 0.0 collective-permute-done.2.down_ref
  49.6 33.3 %all-to-all-done = bf16[64,288,128]{2,1,0:T(8,128)(2,1)} async-done(((bf16[64,288,128]{2,1,0:T(8,128)(2,1)}), bf16[64,288,128]{2,1,0:T(8,128)(2,1)}, u32[]{:S(2)}, u32[]{:S(2)}) %all-to-all-start) | async-done | bytes 4718624 | tf_op jit(solution)/shard_map/all_to_all | solution.py:295
  82.9 0.0 copy-done.2
  82.9 18.6 %expert.1 = bf16[576,32,128]{2,1,0:T(8,128)(2,1)} custom-call(bf16[576,32,128]{2,1,0:T(8,128)(2,1)} %bitcast.4.came_ref, bf16[384,4096]{1,0:T(8,128)(2,1)S(1)} %bitcast.13, bf16[384,4096]{1,0:T(8,128)(2,1)} %bitcast.18, bf16[768,2048]{1,0:T(8,128)(2,1)} %bitcast.20, bf16[384,4096]{1,0:T(8,128)(2,1)} %get-tuple-element.12.gate_other_ref, ...), custom_call_target="tpu_custom_call" | custom-call | flops 10871635968 | bytes 28311552 | tf_op jit(solution)/shard_map/expert/pallas_call | solution.py:233
  101.5 0.0 copy-start
  101.5 0.0 copy-start.1
  101.5 39.7 %all_to_all.10 = bf16[64,288,128]{2,1,0:T(8,128)(2,1)S(1)} all-to-all(bf16[64,288,128]{2,1,0:T(8,128)(2,1)} %bitcast.15), channel_id=1, replica_groups=mesh['fsdp'=2,'expert'=64] {'expert'}, dimensions={0} | all-to-all | bytes 9437184 | tf_op jit(solution)/shard_map/all_to_all | solution.py:295
  141.2 0.0 copy-done
  141.3 0.0 copy-done.1
  141.3 3.2 %combine.1 = bf16[64,4096]{1,0:T(8,128)(2,1)} custom-call(s32[8,128]{1,0:T(8,128)S(1)} %copy-done.1, f32[8,64]{1,0:T(8,128)S(1)} %bitcast.11, bf16[576,32,128]{2,1,0:T(8,128)(2,1)S(1)} %bitcast.10), custom_call_target="tpu_custom_call" | custom-call | tf_op jit(solution)/shard_map/combine/pallas_call | solution.py:282
  (1 shorter events, 0.0 us)
Async XLA Ops:
  0.0 49.6 %collective-permute-start = (bf16[384,4096]{1,0:T(8,128)(2,1)}, bf16[384,4096]{1,0:T(8,128)(2,1)}, u32[]{:S(2)}, u32[]{:S(2)}) collective-permute-start(bf16[384,4096]{1,0:T(8,128)(2,1)} %bitcast.12), channel_id=1, source_target_pairs={{0,64},{64,0},{1,65},{65,1},{2,66},{66,2},{3,67},{67,3},{4,68},{68... | collective-permute-start | bytes 9437192 | tf_op jit(solution)/shard_map/ppermute | solution.py:121
  1.4 48.2 %collective-permute-start.1 = (bf16[384,4096]{1,0:T(8,128)(2,1)}, bf16[384,4096]{1,0:T(8,128)(2,1)}, u32[]{:S(2)}, u32[]{:S(2)}) collective-permute-start(bf16[384,4096]{1,0:T(8,128)(2,1)} %bitcast.17), channel_id=1, source_target_pairs={{0,64},{64,0},{1,65},{65,1},{2,66},{66,2},{3,67},{67,3},{4,68},{68... | collective-permute-start | bytes 9437192 | tf_op jit(solution)/shard_map/ppermute | solution.py:121
  1.4 48.2 %collective-permute-start.2 = (bf16[768,2048]{1,0:T(8,128)(2,1)}, bf16[768,2048]{1,0:T(8,128)(2,1)}, u32[]{:S(2)}, u32[]{:S(2)}) collective-permute-start(bf16[768,2048]{1,0:T(8,128)(2,1)} %bitcast.19), channel_id=1, source_target_pairs={{0,64},{64,0},{1,65},{65,1},{2,66},{66,2},{3,67},{67,3},{4,68},{68... | collective-permute-start | bytes 9437192 | tf_op jit(solution)/shard_map/ppermute | solution.py:121
  37.9 45.0 %all-to-all-start = ((bf16[64,288,128]{2,1,0:T(8,128)(2,1)}), bf16[64,288,128]{2,1,0:T(8,128)(2,1)}, u32[]{:S(2)}, u32[]{:S(2)}) async-start(bf16[64,288,128]{2,1,0:T(8,128)(2,1)} %bitcast.14), calls=%async_computation | async-start | bytes 9437184 | tf_op jit(solution)/shard_map/all_to_all | solution.py:295
  49.6 33.4 %copy-start.2 = (bf16[1,384,4096]{2,1,0:T(8,128)(2,1)S(1)}, bf16[1,384,4096]{2,1,0:T(8,128)(2,1)}, u32[]{:S(2)}) copy-start(bf16[1,384,4096]{2,1,0:T(8,128)(2,1)} %param.9) | copy-start | bytes 9437188
  101.5 39.7 %copy-start = (f32[64,8]{0,1:T(8,128)S(1)}, f32[64,8]{0,1:T(8,128)}, u32[]{:S(2)}) copy-start(f32[64,8]{0,1:T(8,128)} %param.8) | copy-start | bytes 6148
  101.5 39.7 %copy-start.1 = (s32[8,128]{1,0:T(8,128)S(1)}, s32[8,128]{1,0:T(8,128)}, u32[]{:S(2)}) copy-start(s32[8,128]{1,0:T(8,128)} %get-tuple-element.10.place_ref) | copy-start | bytes 12292

commit v5 on v4

--- a/solution.py
+++ b/solution.py
@@ -11,12 +11,13 @@
 ROW_BLOCK = 64
 FF_BLOCK = 256
 PIECE = 128
+PRODUCT = 512
 COLUMN_BLOCK = 2048
-STAGGER = 700
-EXPERT_GROUP = 8
+STAGGER = 696
+EXPERT_GROUP = 4
 DISPATCH_LIMIT = 60 * 1024 * 1024
 SMALL_LIMIT = 14 * 1024 * 1024
-EXPERT_LIMIT = 48 * 1024 * 1024
+EXPERT_LIMIT = 50 * 1024 * 1024
 
 
 def padded(parts):
@@ -50,13 +51,10 @@
     table_ref[...] = table.astype(jnp.int32)
     copy = pltpu.make_async_copy(table_ref, where_ref, table_sem)
     copy.start()
-    place_ref[...] = lax.fori_loop(
+    waited = lax.fori_loop(
         0, late_ref[0], lambda i, a: jnp.sin(a) * 0.5 + 1.0,
         jnp.ones(place_ref.shape, jnp.float32)).astype(jnp.int32)
-    start = rank + (name * capacity).astype(jnp.float32)
-    for k in range(top_count):
-        place = jnp.sum(jnp.where(ids[k:k + 1] == name, start, 0.0), axis=0, keepdims=True)
-        place_ref[k:k + 1, :tok_count] = place.astype(jnp.int32)
+    place_ref[...] = waited
     for part in range(parts):
         wide_ref[pl.ds(part, tok_count, stride=pitch), :] = (
             tokens_ref[:, part * LANES:(part + 1) * LANES].astype(jnp.float32))
@@ -73,12 +71,17 @@
 
     @pl.loop(0, experts_count // EXPERT_GROUP)
     def _(g):
-        @pl.loop(0, EXPERT_GROUP)
+        @pl.loop(0, EXPERT_GROUP, unroll=4)
         def _(i):
             e = g * EXPERT_GROUP + i
             for slot in range(capacity):
                 stage_ref[e * capacity + slot] = rows_ref[where_ref[e, slot]]
         send(g).start()
+
+    start = rank + (name * capacity).astype(jnp.float32)
+    for k in range(top_count):
+        place = jnp.sum(jnp.where(ids[k:k + 1] == name, start, 0.0), axis=0, keepdims=True)
+        place_ref[k:k + 1, :tok_count] = place.astype(jnp.int32)
 
     @pl.loop(0, experts_count // EXPERT_GROUP)
     def _(g):
@@ -133,9 +136,8 @@
 
 
 def expert_kernel(came_ref, gate_ref, up_ref, down_ref, gate_other_ref, up_other_ref,
-                  down_other_ref, out_ref, held_ref, gate_all_ref, up_all_ref, down_all_ref,
-                  wide_ref, rows_ref, hidden_ref, result_ref, came_sem, gate_sem, up_sem,
-                  down_sem):
+                  down_other_ref, out_ref, held_ref, both_ref, down_all_ref,
+                  wide_ref, rows_ref, hidden_ref, result_ref, came_sem, both_sem, down_sem):
     count, parts = came_ref.shape[0], came_ref.shape[1]
     half_ff, width = gate_ref.shape
     columns = down_ref.shape[1]
@@ -151,15 +153,16 @@
     def _(b):
         fetch(b).start()
 
-    pairs = ((gate_ref, gate_other_ref, gate_all_ref, gate_sem),
-             (up_ref, up_other_ref, up_all_ref, up_sem))
+    pairs = ((gate_ref, gate_other_ref), (up_ref, up_other_ref))
     pieces = []
     for low in range(0, 2 * half_ff, PIECE):
         at, own = low % half_ff, low < half_ff
-        for first, second, full, sem in pairs:
+        step, inside = low // FF_BLOCK, low % FF_BLOCK
+        for which, (first, second) in enumerate(pairs):
+            to = (2 * step + which) * FF_BLOCK + inside
             pieces.append(pltpu.make_async_copy(
                 (first if own else second).at[at:at + PIECE],
-                full.at[low:low + PIECE], sem.at[low // PIECE]))
+                both_ref.at[to:to + PIECE], both_sem.at[len(pieces)]))
     per_step = len(pairs) * FF_BLOCK // PIECE
     down_copies = []
     for which, (part, index) in enumerate(((down_ref, mine), (down_other_ref, 1 - mine))):
@@ -194,11 +197,9 @@
         for copy in pieces[step * per_step:(step + 1) * per_step]:
             copy.wait()
         low = step * FF_BLOCK
-        rows = rows_ref[...]
-        gate = lax.dot_general(rows, gate_all_ref[low:low + FF_BLOCK], contract,
+        both = lax.dot_general(rows_ref[...], both_ref[2 * low:2 * (low + FF_BLOCK)], contract,
                                preferred_element_type=jnp.float32)
-        up = lax.dot_general(rows, up_all_ref[low:low + FF_BLOCK], contract,
-                             preferred_element_type=jnp.float32)
+        gate, up = both[:, :FF_BLOCK], both[:, FF_BLOCK:]
         hidden = gate / (1.0 + jnp.exp(-gate)) * up
         hidden_ref[:, low:low + FF_BLOCK] = hidden.astype(hidden_ref.dtype)
     for copy in down_copies:
@@ -206,22 +207,32 @@
 
     out_parts = COLUMN_BLOCK // LANES
     out_pitch = padded(out_parts)
-    for block in range(width // COLUMN_BLOCK):
-        for piece in range(COLUMN_BLOCK // 256):
-            low = block * COLUMN_BLOCK + piece * 256
-            result = jnp.dot(hidden_ref[...], down_all_ref[:, low:low + 256],
+    products = COLUMN_BLOCK // PRODUCT
+    column_blocks = width // COLUMN_BLOCK
+
+    def convert(block, at, rows):
+        for row in range(rows):
+            first = (at + row) * out_pitch
+            if not isinstance(first, int):
+                first = pl.multiple_of(first, 8)
+            out_ref[at + row, block * out_parts:(block + 1) * out_parts] = (
+                result_ref[block % 2, pl.ds(first, out_parts), :].astype(out_ref.dtype))
+
+    for block in range(column_blocks):
+        for piece in range(products):
+            low = block * COLUMN_BLOCK + piece * PRODUCT
+            result = jnp.dot(hidden_ref[...], down_all_ref[:, low:low + PRODUCT],
                              preferred_element_type=jnp.float32)
-            for half in range(2):
-                result_ref[pl.ds(2 * piece + half, count, stride=out_pitch), :] = (
-                    result[:, half * LANES:(half + 1) * LANES])
-
-        @pl.loop(0, count // ROW_BLOCK)
-        def _(b):
-            at = pl.multiple_of(b * ROW_BLOCK, ROW_BLOCK)
-            for row in range(ROW_BLOCK):
-                first = pl.multiple_of((at + row) * out_pitch, 8)
-                out_ref[at + row, block * out_parts:(block + 1) * out_parts] = (
-                    result_ref[pl.ds(first, out_parts), :].astype(out_ref.dtype))
+            for part in range(PRODUCT // LANES):
+                at = piece * (PRODUCT // LANES) + part
+                result_ref[block % 2, pl.ds(at, count, stride=out_pitch), :] = (
+                    result[:, part * LANES:(part + 1) * LANES])
+            if block > 0:
+                convert(block - 1, piece * (count // products), count // products)
+
+    @pl.loop(0, count // ROW_BLOCK)
+    def _(b):
+        convert(column_blocks - 1, b * ROW_BLOCK, ROW_BLOCK)
 
 
 def expert(came, own, other):
@@ -237,16 +248,14 @@
         out_specs=pl.BlockSpec(memory_space=pltpu.VMEM),
         scratch_shapes=[
             pltpu.VMEM(came.shape, dtype),
-            pltpu.VMEM((ff, width), dtype),
-            pltpu.VMEM((ff, width), dtype),
+            pltpu.VMEM((2 * ff, width), dtype),
             pltpu.VMEM((ff, width), dtype),
             pltpu.VMEM((ROW_BLOCK * padded(parts), LANES), jnp.float32),
             pltpu.VMEM((count, width), dtype),
             pltpu.VMEM((count, ff), dtype),
-            pltpu.VMEM((count * padded(COLUMN_BLOCK // LANES), LANES), jnp.float32),
+            pltpu.VMEM((2, count * padded(COLUMN_BLOCK // LANES), LANES), jnp.float32),
             pltpu.SemaphoreType.DMA((count // ROW_BLOCK,)),
-            pltpu.SemaphoreType.DMA((steps,)),
-            pltpu.SemaphoreType.DMA((steps,)),
+            pltpu.SemaphoreType.DMA((2 * steps,)),
             pltpu.SemaphoreType.DMA((4,)),
         ],
         compiler_params=pltpu.CompilerParams(vmem_limit_bytes=EXPERT_LIMIT),
@@ -262,11 +271,13 @@
     parts = back_ref.shape[1]
     pitch = padded(parts)
 
-    @pl.loop(0, tok_count)
+    @pl.loop(0, tok_count, unroll=4)
     def _(t):
-        total = jnp.zeros((parts, LANES), jnp.float32)
-        for k in range(top_count):
-            total += share_ref[k, t] * back_ref[place_ref[k, t]].astype(jnp.float32)
+        terms = [share_ref[k, t] * back_ref[place_ref[k, t]].astype(jnp.float32)
+                 for k in range(top_count)]
+        while len(terms) > 1:
+            terms = [left + right for left, right in zip(terms[::2], terms[1::2])]
+        total = terms[0]
         total_ref[pl.ds(pl.multiple_of(t * pitch, 8), parts), :] = total
 
     for part in range(parts):

time: 145 us -> 144 us (level)
  no operation moved by 1% of the time
where the time goes in v5:
time: 144 us; the launch traced here: 143 us
  Pallas kernels  57 us (40%)
  blocking collectives  39.4 us (27%)
  waiting for transfers between devices  33.3 us (23%)
  starting transfers between devices  13.6 us (9%)
    all_to_all x1, blocking collectives, exchange(): lax.all_to_all(sent, 'expert', split_axis=0, concat_axis=0, tiled=True)  39.4 us
    pallas_call x1, Pallas kernels, dispatch(): pl.pallas_call(functools.partial(dispatch_kernel, capacity), out_shape=(j...  35.8 us
    all_to_all x1, waiting for transfers between devices, exchange(): lax.all_to_all(sent, 'expert', split_axis=0, concat_axis=0, tiled=True)  33.3 us
    pallas_call x1, Pallas kernels, expert(): pl.pallas_call(expert_kernel, out_shape=jax.ShapeDtypeStruct(came.shape,...  18.5 us
    all_to_all x1, starting transfers between devices, exchange(): lax.all_to_all(sent, 'expert', split_axis=0, concat_axis=0, tiled=True)  11.6 us
  transfers between devices with their start and end apart: 4, of which 1 were waited for; matrix products, arithmetic and copies ran while one was open for 0% of the time, Pallas kernels for 25%

profile of v5, /device:TPU:1, one launch (start us, length us, event | category | flops | bytes accessed | tf_op | source)
XLA Modules:
  0.0 143.4 jit_solution(16959717569400450551)
XLA Ops:
  0.0 1.4 collective-permute-start
  1.4 0.0 collective-permute-start.1
  1.4 0.5 collective-permute-start.2
  1.9 35.8 %dispatch.1 = (bf16[576,32,128]{2,1,0:T(8,128)(2,1)}, s32[8,128]{1,0:T(8,128)}) custom-call(s32[1]{0:T(128)} %bitcast.late_ref, s32[8,64]{1,0:T(8,128)} %bitcast.16, bf16[64,4096]{1,0:T(8,128)(2,1)} %tokens_ref.1), custom_call_target="tpu_custom_call" | custom-call | tf_op jit(solution)/shard_map/dispatch/pallas_call | solution.py:97
  37.7 11.6 %all-to-all-start = ((bf16[64,288,128]{2,1,0:T(8,128)(2,1)}), bf16[64,288,128]{2,1,0:T(8,128)(2,1)}, u32[]{:S(2)}, u32[]{:S(2)}) async-start(bf16[64,288,128]{2,1,0:T(8,128)(2,1)} %bitcast.14), calls=%async_computation | async-start | bytes 9437184 | tf_op jit(solution)/shard_map/all_to_all | solution.py:306
  49.3 0.0 copy-start.2
  49.4 0.0 collective-permute-done.gate_ref
  49.4 0.0 collective-permute-done.1.up_ref
  49.4 0.0 collective-permute-done.2.down_ref
  49.4 33.3 %all-to-all-done = bf16[64,288,128]{2,1,0:T(8,128)(2,1)} async-done(((bf16[64,288,128]{2,1,0:T(8,128)(2,1)}), bf16[64,288,128]{2,1,0:T(8,128)(2,1)}, u32[]{:S(2)}, u32[]{:S(2)}) %all-to-all-start) | async-done | bytes 4718624 | tf_op jit(solution)/shard_map/all_to_all | solution.py:306
  82.7 0.0 copy-done.2
  82.7 18.5 %expert.1 = bf16[576,32,128]{2,1,0:T(8,128)(2,1)} custom-call(bf16[576,32,128]{2,1,0:T(8,128)(2,1)} %bitcast.4.came_ref, bf16[384,4096]{1,0:T(8,128)(2,1)S(1)} %bitcast.13, bf16[384,4096]{1,0:T(8,128)(2,1)} %bitcast.18, bf16[768,2048]{1,0:T(8,128)(2,1)} %bitcast.20, bf16[384,4096]{1,0:T(8,128)(2,1)} %get-tuple-element.12.gate_other_ref, ...), custom_call_target="tpu_custom_call" | custom-call | flops 10871635968 | bytes 28311552 | tf_op jit(solution)/shard_map/expert/pallas_call | solution.py:244
  101.2 0.0 copy-start
  101.2 0.0 copy-start.1
  101.3 39.4 %all_to_all.10 = bf16[64,288,128]{2,1,0:T(8,128)(2,1)S(1)} all-to-all(bf16[64,288,128]{2,1,0:T(8,128)(2,1)} %bitcast.15), channel_id=1, replica_groups=mesh['fsdp'=2,'expert'=64] {'expert'}, dimensions={0} | all-to-all | bytes 9437184 | tf_op jit(solution)/shard_map/all_to_all | solution.py:306
  140.7 0.0 copy-done
  140.7 0.0 copy-done.1
  140.7 2.7 %combine.1 = bf16[64,4096]{1,0:T(8,128)(2,1)} custom-call(s32[8,128]{1,0:T(8,128)S(1)} %copy-done.1, f32[8,64]{1,0:T(8,128)S(1)} %bitcast.11, bf16[576,32,128]{2,1,0:T(8,128)(2,1)S(1)} %bitcast.10), custom_call_target="tpu_custom_call" | custom-call | tf_op jit(solution)/shard_map/combine/pallas_call | solution.py:293
  (1 shorter events, 0.0 us)
Async XLA Ops:
  0.0 49.4 %collective-permute-start = (bf16[384,4096]{1,0:T(8,128)(2,1)}, bf16[384,4096]{1,0:T(8,128)(2,1)}, u32[]{:S(2)}, u32[]{:S(2)}) collective-permute-start(bf16[384,4096]{1,0:T(8,128)(2,1)} %bitcast.12), channel_id=1, source_target_pairs={{0,64},{64,0},{1,65},{65,1},{2,66},{66,2},{3,67},{67,3},{4,68},{68... | collective-permute-start | bytes 9437192 | tf_op jit(solution)/shard_map/ppermute | solution.py:124
  1.4 47.9 %collective-permute-start.1 = (bf16[384,4096]{1,0:T(8,128)(2,1)}, bf16[384,4096]{1,0:T(8,128)(2,1)}, u32[]{:S(2)}, u32[]{:S(2)}) collective-permute-start(bf16[384,4096]{1,0:T(8,128)(2,1)} %bitcast.17), channel_id=1, source_target_pairs={{0,64},{64,0},{1,65},{65,1},{2,66},{66,2},{3,67},{67,3},{4,68},{68... | collective-permute-start | bytes 9437192 | tf_op jit(solution)/shard_map/ppermute | solution.py:124
  1.4 48.0 %collective-permute-start.2 = (bf16[768,2048]{1,0:T(8,128)(2,1)}, bf16[768,2048]{1,0:T(8,128)(2,1)}, u32[]{:S(2)}, u32[]{:S(2)}) collective-permute-start(bf16[768,2048]{1,0:T(8,128)(2,1)} %bitcast.19), channel_id=1, source_target_pairs={{0,64},{64,0},{1,65},{65,1},{2,66},{66,2},{3,67},{67,3},{4,68},{68... | collective-permute-start | bytes 9437192 | tf_op jit(solution)/shard_map/ppermute | solution.py:124
  37.7 45.0 %all-to-all-start = ((bf16[64,288,128]{2,1,0:T(8,128)(2,1)}), bf16[64,288,128]{2,1,0:T(8,128)(2,1)}, u32[]{:S(2)}, u32[]{:S(2)}) async-start(bf16[64,288,128]{2,1,0:T(8,128)(2,1)} %bitcast.14), calls=%async_computation | async-start | bytes 9437184 | tf_op jit(solution)/shard_map/all_to_all | solution.py:306
  49.3 33.4 %copy-start.2 = (bf16[1,384,4096]{2,1,0:T(8,128)(2,1)S(1)}, bf16[1,384,4096]{2,1,0:T(8,128)(2,1)}, u32[]{:S(2)}) copy-start(bf16[1,384,4096]{2,1,0:T(8,128)(2,1)} %param.9) | copy-start | bytes 9437188
  101.2 39.5 %copy-start = (f32[64,8]{0,1:T(8,128)S(1)}, f32[64,8]{0,1:T(8,128)}, u32[]{:S(2)}) copy-start(f32[64,8]{0,1:T(8,128)} %param.8) | copy-start | bytes 6148
  101.2 39.5 %copy-start.1 = (s32[8,128]{1,0:T(8,128)S(1)}, s32[8,128]{1,0:T(8,128)}, u32[]{:S(2)}) copy-start(s32[8,128]{1,0:T(8,128)} %get-tuple-element.10.place_ref) | copy-start | bytes 12292

commit v6 on v5

--- a/solution.py
+++ b/solution.py
@@ -13,7 +13,7 @@
 PIECE = 128
 PRODUCT = 512
 COLUMN_BLOCK = 2048
-STAGGER = 696
+STAGGER = 654
 EXPERT_GROUP = 4
 DISPATCH_LIMIT = 60 * 1024 * 1024
 SMALL_LIMIT = 14 * 1024 * 1024
@@ -311,7 +311,7 @@
     experts_count = lax.axis_size("expert") * gate_weight.shape[0]
     tok_count, top_count = expert_ids.shape
     capacity = tok_count * top_count // experts_count + 1
-    late = (lax.axis_index("fsdp") * STAGGER).astype(jnp.int32).reshape(1)
+    late = ((1 - lax.axis_index("fsdp")) * STAGGER).astype(jnp.int32).reshape(1)
     sent, place = dispatch(late, expert_ids.T, tokens, experts_count, capacity)
     came = exchange(sent, experts_count)
     own = (gate_weight[0], up_weight[0], down_weight[0])

time: 144 us -> 143 us (level)
  the two profiles are of different devices: /device:TPU:1 before, /device:TPU:0 now
where the time goes in v6:
time: 143 us
  Pallas kernels  55.1 us (39%)
  blocking collectives  40.8 us (29%)
  waiting for transfers between devices  34.5 us (24%)
  starting transfers between devices  12.4 us (9%)
    all_to_all x1, blocking collectives, exchange(): lax.all_to_all(sent, 'expert', split_axis=0, concat_axis=0, tiled=True)  40.8 us
    all_to_all x1, waiting for transfers between devices, exchange(): lax.all_to_all(sent, 'expert', split_axis=0, concat_axis=0, tiled=True)  34.5 us
    pallas_call x1, Pallas kernels, dispatch(): pl.pallas_call(functools.partial(dispatch_kernel, capacity), out_shape=(j...  33.9 us
    pallas_call x1, Pallas kernels, expert(): pl.pallas_call(expert_kernel, out_shape=jax.ShapeDtypeStruct(came.shape,...  18.5 us
    all_to_all x1, starting transfers between devices, exchange(): lax.all_to_all(sent, 'expert', split_axis=0, concat_axis=0, tiled=True)  11.9 us
  transfers between devices with their start and end apart: 4, of which 1 were waited for; matrix products, arithmetic and copies ran while one was open for 0% of the time, Pallas kernels for 24%

profile of v6, /device:TPU:0, one launch (start us, length us, event | category | flops | bytes accessed | tf_op | source)
XLA Modules:
  0.0 142.9 jit_solution(8697021674266098410)
XLA Ops:
  0.0 0.0 collective-permute-start
  0.0 0.5 collective-permute-start.1
  0.5 0.0 collective-permute-start.2
  0.5 33.9 %dispatch.1 = (bf16[576,32,128]{2,1,0:T(8,128)(2,1)}, s32[8,128]{1,0:T(8,128)}) custom-call(s32[1]{0:T(128)} %bitcast.late_ref, s32[8,64]{1,0:T(8,128)} %bitcast.16, bf16[64,4096]{1,0:T(8,128)(2,1)} %tokens_ref.1), custom_call_target="tpu_custom_call" | custom-call | tf_op jit(solution)/shard_map/dispatch/pallas_call | solution.py:97
  34.4 11.9 %all-to-all-start = ((bf16[64,288,128]{2,1,0:T(8,128)(2,1)}), bf16[64,288,128]{2,1,0:T(8,128)(2,1)}, u32[]{:S(2)}, u32[]{:S(2)}) async-start(bf16[64,288,128]{2,1,0:T(8,128)(2,1)} %bitcast.14), calls=%async_computation | async-start | bytes 9437184 | tf_op jit(solution)/shard_map/all_to_all | solution.py:306
  46.3 0.0 copy-start.2
  46.3 0.0 collective-permute-done.gate_ref
  46.4 0.0 collective-permute-done.1.up_ref
  46.4 0.0 collective-permute-done.2.down_ref
  46.4 34.5 %all-to-all-done = bf16[64,288,128]{2,1,0:T(8,128)(2,1)} async-done(((bf16[64,288,128]{2,1,0:T(8,128)(2,1)}), bf16[64,288,128]{2,1,0:T(8,128)(2,1)}, u32[]{:S(2)}, u32[]{:S(2)}) %all-to-all-start) | async-done | bytes 4718624 | tf_op jit(solution)/shard_map/all_to_all | solution.py:306
  80.8 0.0 copy-done.2
  80.8 18.5 %expert.1 = bf16[576,32,128]{2,1,0:T(8,128)(2,1)} custom-call(bf16[576,32,128]{2,1,0:T(8,128)(2,1)} %bitcast.4.came_ref, bf16[384,4096]{1,0:T(8,128)(2,1)S(1)} %bitcast.13, bf16[384,4096]{1,0:T(8,128)(2,1)} %bitcast.18, bf16[768,2048]{1,0:T(8,128)(2,1)} %bitcast.20, bf16[384,4096]{1,0:T(8,128)(2,1)} %get-tuple-element.12.gate_other_ref, ...), custom_call_target="tpu_custom_call" | custom-call | flops 10871635968 | bytes 28311552 | tf_op jit(solution)/shard_map/expert/pallas_call | solution.py:244
  99.4 0.0 copy-start
  99.4 0.0 copy-start.1
  99.4 40.8 %all_to_all.10 = bf16[64,288,128]{2,1,0:T(8,128)(2,1)S(1)} all-to-all(bf16[64,288,128]{2,1,0:T(8,128)(2,1)} %bitcast.15), channel_id=1, replica_groups=mesh['fsdp'=2,'expert'=64] {'expert'}, dimensions={0} | all-to-all | bytes 9437184 | tf_op jit(solution)/shard_map/all_to_all | solution.py:306
  140.2 0.0 copy-done
  140.2 0.0 copy-done.1
  140.2 2.7 %combine.1 = bf16[64,4096]{1,0:T(8,128)(2,1)} custom-call(s32[8,128]{1,0:T(8,128)S(1)} %copy-done.1, f32[8,64]{1,0:T(8,128)S(1)} %bitcast.11, bf16[576,32,128]{2,1,0:T(8,128)(2,1)S(1)} %bitcast.10), custom_call_target="tpu_custom_call" | custom-call | tf_op jit(solution)/shard_map/combine/pallas_call | solution.py:293
  (1 shorter events, 0.0 us)
Async XLA Ops:
  0.0 46.3 %collective-permute-start = (bf16[384,4096]{1,0:T(8,128)(2,1)}, bf16[384,4096]{1,0:T(8,128)(2,1)}, u32[]{:S(2)}, u32[]{:S(2)}) collective-permute-start(bf16[384,4096]{1,0:T(8,128)(2,1)} %bitcast.12), channel_id=1, source_target_pairs={{0,64},{64,0},{1,65},{65,1},{2,66},{66,2},{3,67},{67,3},{4,68},{68... | collective-permute-start | bytes 9437192 | tf_op jit(solution)/shard_map/ppermute | solution.py:124
  0.0 46.4 %collective-permute-start.1 = (bf16[384,4096]{1,0:T(8,128)(2,1)}, bf16[384,4096]{1,0:T(8,128)(2,1)}, u32[]{:S(2)}, u32[]{:S(2)}) collective-permute-start(bf16[384,4096]{1,0:T(8,128)(2,1)} %bitcast.17), channel_id=1, source_target_pairs={{0,64},{64,0},{1,65},{65,1},{2,66},{66,2},{3,67},{67,3},{4,68},{68... | collective-permute-start | bytes 9437192 | tf_op jit(solution)/shard_map/ppermute | solution.py:124
  0.5 45.9 %collective-permute-start.2 = (bf16[768,2048]{1,0:T(8,128)(2,1)}, bf16[768,2048]{1,0:T(8,128)(2,1)}, u32[]{:S(2)}, u32[]{:S(2)}) collective-permute-start(bf16[768,2048]{1,0:T(8,128)(2,1)} %bitcast.19), channel_id=1, source_target_pairs={{0,64},{64,0},{1,65},{65,1},{2,66},{66,2},{3,67},{67,3},{4,68},{68... | collective-permute-start | bytes 9437192 | tf_op jit(solution)/shard_map/ppermute | solution.py:124
  34.4 46.4 %all-to-all-start = ((bf16[64,288,128]{2,1,0:T(8,128)(2,1)}), bf16[64,288,128]{2,1,0:T(8,128)(2,1)}, u32[]{:S(2)}, u32[]{:S(2)}) async-start(bf16[64,288,128]{2,1,0:T(8,128)(2,1)} %bitcast.14), calls=%async_computation | async-start | bytes 9437184 | tf_op jit(solution)/shard_map/all_to_all | solution.py:306
  46.3 34.5 %copy-start.2 = (bf16[1,384,4096]{2,1,0:T(8,128)(2,1)S(1)}, bf16[1,384,4096]{2,1,0:T(8,128)(2,1)}, u32[]{:S(2)}) copy-start(bf16[1,384,4096]{2,1,0:T(8,128)(2,1)} %param.9) | copy-start | bytes 9437188
  99.4 40.8 %copy-start = (f32[64,8]{0,1:T(8,128)S(1)}, f32[64,8]{0,1:T(8,128)}, u32[]{:S(2)}) copy-start(f32[64,8]{0,1:T(8,128)} %param.8) | copy-start | bytes 6148
  99.4 40.8 %copy-start.1 = (s32[8,128]{1,0:T(8,128)S(1)}, s32[8,128]{1,0:T(8,128)}, u32[]{:S(2)}) copy-start(s32[8,128]{1,0:T(8,128)} %get-tuple-element.10.place_ref) | copy-start | bytes 12292
